TPU v7x, 128 devices: a whole 4x4x4 slice. The times are simulated.
128 devices in a mesh: gx: 16 (over y_lo, z, core), gy: 8 (over x, y_hi).
Axes of the slice: x: 4, y: 4 (y_hi: 2, y_lo: 2; y = y_hi * 2 + y_lo), z: 4, core: 2. Of those that a mesh axis runs over, the one named last changes fastest.
Arguments:
- mass: float32 [5, 512, 2048], P(None, 'gy', 'gx'), may hold values from 0.05 to 1
- tracer: float32 [5, 7, 512, 2048], P(None, None, 'gy', 'gx'), may hold values from -4 to 4
- uvel: float32 [512, 2048], P('gy', 'gx'), may hold values from -0.45 to 0.45
- vvel: float32 [512, 2048], P('gy', 'gx'), may hold values from -0.45 to 0.45
- case_east: int32 [512, 2048], P('gy', 'gx'), may hold values from 0 to 2
- case_north: int32 [512, 2048], P('gy', 'gx'), may hold values from 0 to 2
- ice_blocks: int32 [16, 64], P('gy', 'gx'), may hold values 0 or 1
Outputs:
- mass_out: float32 [5, 512, 2048], P(None, 'gy', 'gx')
- tracer_out: float32 [5, 7, 512, 2048], P(None, None, 'gy', 'gx')
Inputs may be any that keep to these rules, and one draw needn't show every extreme that they name: `case_east`: 0 means no corner triangle, 1 the lower corner, 2 the upper corner. `case_north`: 0 means no corner triangle, 1 the western corner, 2 the eastern corner.
All inputs are finite; a program needn't handle non-finite values. No bound on the sum of `ice_blocks` on one device may be relied on, other than what follows from the above.
Results may differ from a plain program's by a relative error of at most 0.0003.
Values sent between devices are 32-bit elements; how exact they have to be, the bound alone decides.
A program may use at most 128 MiB of HBM per device.

v0:
```python
import jax
import jax.numpy as jnp
from jax import lax
from jax.sharding import PartitionSpec as P

STEPS = 2


mass_floor = 0.1


def from_partner(shard, axis, apart):
    return lax.ppermute(shard, axis, [(i, i ^ 1 << apart) for i in range(lax.axis_size(axis))])


def extended_2(block, sides, width):
    for axis, dim in sides:
        count = lax.axis_size(axis)
        forward = [(i, i + 1) for i in range(count - 1)]
        forward.append((count - 1, 0))
        backward = [(target, source) for source, target in forward]
        low = lax.ppermute(
            lax.slice_in_dim(block, block.shape[dim] - width, None, axis=dim), axis, forward
        )
        high = lax.ppermute(lax.slice_in_dim(block, 0, width, axis=dim), axis, backward)
        block = jnp.concatenate([low, block, high], axis=dim)
    return block


def region(region_area, normal_pos, trans_pos, cell):
    values, grad_normal, grad_trans = cell
    centre_val = values + grad_normal * normal_pos + grad_trans * trans_pos
    carried = region_area * centre_val[0]
    return jnp.concatenate([carried[None], carried[None] * centre_val[1:]], axis=0)


def choose(forward, when_true, when_false):
    return tuple(
        (
            jnp.where(forward, left_arr, right_arr)
            for left_arr, right_arr in zip(when_true, when_false)
        )
    )


def edge_flux(
    normal_speed,
    low_speed,
    high_speed,
    case_id,
    low_side,
    high_side,
    low_below,
    low_above,
    high_below,
    high_above,
):
    forward = normal_speed > 0.0
    signs = jnp.where(forward, 1.0, -1.0)
    reach = jnp.abs(normal_speed)
    source = choose(forward, low_side, high_side)
    beneath = choose(forward, low_below, high_below)
    overhead = choose(forward, low_above, high_above)
    summed = region(reach, signs * (0.5 - 0.5 * reach), 0.0, source)
    tri_normal = signs * (0.5 - reach / 3.0)
    low_area = jnp.where(case_id == 1, 0.5 * reach * low_speed, 0.0)
    low_offset = 0.5 - low_speed / 3.0
    summed = (
        summed
        + region(low_area, tri_normal, low_offset, beneath)
        - region(low_area, tri_normal, -low_offset, source)
    )
    high_area = jnp.where(case_id == 2, 0.5 * reach * high_speed, 0.0)
    high_offset = 0.5 - high_speed / 3.0
    summed = (
        summed
        + region(high_area, tri_normal, -high_offset, overhead)
        - region(high_area, tri_normal, high_offset, source)
    )
    return signs * summed


def category_fluxes(
    values, slopes, u_ext, v_ext, case_east_al, case_north_al, east_from, north_from
):
    height = values.shape[1] - 2
    breadth = values.shape[2] - 2

    def along_x(row_sel, col_sel):
        return (
            values[:, row_sel, col_sel],
            slopes[0][:, row_sel, col_sel],
            slopes[1][:, row_sel, col_sel],
        )

    def along_y(row_sel, col_sel):
        return (
            values[:, row_sel, col_sel],
            slopes[1][:, row_sel, col_sel],
            slopes[0][:, row_sel, col_sel],
        )

    low_cols = slice(east_from + 1, breadth + 1)
    high_cols = slice(east_from + 2, breadth + 2)
    centre = slice(1, height + 1)
    below_rows = slice(0, height)
    above_rows = slice(2, height + 2)
    speed_east = 0.5 * (u_ext[centre, low_cols] + u_ext[below_rows, low_cols])
    east_flux = edge_flux(
        speed_east,
        jnp.abs(v_ext[below_rows, low_cols]),
        jnp.abs(v_ext[centre, low_cols]),
        case_east_al,
        along_x(centre, low_cols),
        along_x(centre, high_cols),
        along_x(below_rows, low_cols),
        along_x(above_rows, low_cols),
        along_x(below_rows, high_cols),
        along_x(above_rows, high_cols),
    )
    low_rows = slice(north_from + 1, height + 1)
    high_rows = slice(north_from + 2, height + 2)
    centre_cols = slice(1, breadth + 1)
    west_cols = slice(0, breadth)
    east_cols = slice(2, breadth + 2)
    speed_north = 0.5 * (v_ext[low_rows, centre_cols] + v_ext[low_rows, west_cols])
    north_flux = edge_flux(
        speed_north,
        jnp.abs(u_ext[low_rows, west_cols]),
        jnp.abs(u_ext[low_rows, centre_cols]),
        case_north_al,
        along_y(low_rows, centre_cols),
        along_y(high_rows, centre_cols),
        along_y(low_rows, west_cols),
        along_y(low_rows, east_cols),
        along_y(high_rows, west_cols),
        along_y(high_rows, east_cols),
    )
    return (east_flux, north_flux)


def all_fluxes(values, slopes, u_ext, v_ext, case_east_al, case_north_al, east_from, north_from):

    def per_category(paired):
        return category_fluxes(
            paired[0], paired[1], u_ext, v_ext, case_east_al, case_north_al, east_from, north_from
        )

    return lax.map(per_category, (values, slopes))


def slope_pair(extended):
    along_lon = 0.5 * (extended[..., 1:-1, 2:] - extended[..., 1:-1, :-2])
    along_lat = 0.5 * (extended[..., 2:, 1:-1] - extended[..., :-2, 1:-1])
    return jnp.stack([along_lon, along_lat], axis=1)


def update(fields, east_flux, north_flux):
    carried = fields[:, 0]
    conserved = jnp.concatenate([carried[:, None], carried[:, None] * fields[:, 1:]], axis=1)
    conserved = (
        conserved
        - (east_flux[..., 1:] - east_flux[..., :-1])
        - (north_flux[..., 1:, :] - north_flux[..., :-1, :])
    )
    new_mass = conserved[:, 0]
    amounts = conserved[:, 1:] / jnp.maximum(new_mass, mass_floor)[:, None]
    return jnp.concatenate([new_mass[:, None], amounts], axis=1)


def fold_strip(strip):
    leading = strip.shape[:-1]
    extent = strip.shape[-1]
    flat_strip = strip.reshape(-1, extent)
    devices_x = lax.axis_size("gx")
    mirrored = flat_strip
    for bit_number in range(devices_x.bit_length() - 1):
        mirrored = from_partner(mirrored, "gx", bit_number)
    return mirrored.reshape(leading + (extent,))[..., ::-1, ::-1]


def mend_rims(extended, margin, factor):
    height = extended.shape[-2] - 2 * margin
    at_bottom = lax.axis_index("gy") == 0
    at_top = lax.axis_index("gy") == lax.axis_size("gy") - 1
    folded = factor * fold_strip(extended[..., height : height + margin, :])
    bottom_rows = jnp.where(at_bottom, 0.0, extended[..., :margin, :])
    top_rows = jnp.where(at_top, folded, extended[..., height + margin :, :])
    return jnp.concatenate(
        [bottom_rows, extended[..., margin : height + margin, :], top_rows], axis=-2
    )


def zero_bottom(extended, margin):
    at_bottom = lax.axis_index("gy") == 0
    bottom_rows = jnp.where(at_bottom, 0.0, extended[..., :margin, :])
    return jnp.concatenate([bottom_rows, extended[..., margin:, :]], axis=-2)


def local_step(deep_fields, deep_aux):
    height = deep_fields.shape[2] - 4
    breadth = deep_fields.shape[3] - 4
    slopes = slope_pair(deep_fields)
    values = deep_fields[..., 1:-1, 1:-1]
    u_ext = deep_aux[0, 0, 1:-1, 1:-1]
    v_ext = deep_aux[0, 1, 1:-1, 1:-1]
    case_east_al = deep_aux[0, 2, 2 : height + 2, 1 : breadth + 2]
    case_north_al = deep_aux[0, 3, 1 : height + 2, 2 : breadth + 2]
    east_flux, north_flux = all_fluxes(
        values, slopes, u_ext, v_ext, case_east_al, case_north_al, -1, -1
    )
    return update(deep_fields[..., 2:-2, 2:-2], east_flux, north_flux)


def owner_step(fields, auxiliary):
    deep_fields, deep_aux = (
        extended_2(fields, (("gy", 2), ("gx", 3)), 2),
        extended_2(auxiliary, (("gy", 2), ("gx", 3)), 2),
    )
    deep_fields = mend_rims(deep_fields, 2, 1.0)
    deep_aux = zero_bottom(deep_aux, 2)
    return local_step(deep_fields, deep_aux)


def per_device(mass, tracer, uvel, vvel, case_east, case_north, ice_blocks):
    height = mass.shape[1]
    breadth = mass.shape[2]
    block_rows = height // ice_blocks.shape[0]
    block_cols = breadth // ice_blocks.shape[1]
    cell_mask = jnp.repeat(jnp.repeat(ice_blocks, block_rows, axis=0), block_cols, axis=1).astype(
        jnp.float32
    )
    fields = jnp.concatenate([(mass * cell_mask)[:, None], tracer], axis=1)
    auxiliary = jnp.stack(
        [uvel, vvel, case_east.astype(jnp.float32), case_north.astype(jnp.float32)]
    )[None]
    for sweep in range(STEPS):
        fields = owner_step(fields, auxiliary)
    return (fields[:, 0], fields[:, 1:])


def solution(mesh):
    placed = (
        P(None, "gy", "gx"),
        P(None, None, "gy", "gx"),
        P("gy", "gx"),
        P("gy", "gx"),
        P("gy", "gx"),
        P("gy", "gx"),
        P("gy", "gx"),
    )
    return jax.shard_map(
        per_device,
        mesh=mesh,
        in_specs=placed,
        out_specs=(P(None, "gy", "gx"), P(None, None, "gy", "gx")),
        check_vma=False,
    )
```

profile of v0, /device:TPU:6, one launch (start us, length us, event | category | flops | bytes accessed | tf_op | source)
XLA Modules:
  0.0 207.5 jit_solution(7460064438038395480)
XLA Ops:
  3.8 3.3 %collective-permute-start.4 = (f32[5,8,2,128]{3,2,1,0:T(2,128)S(1)}, f32[5,8,2,128]{3,2,1,0:T(2,128)S(1)}, u32[]{:S(2)}, u32[]{:S(2)}) collective-permute-start(f32[5,8,2,128]{3,2,1,0:T(2,128)S(1)} %get-tuple-element.553), channel_id=1, source_target_pairs={{0,1},{1,2},{2,3},{3,4},{4,5},{5,6},{6,7},{7,0},{8,9},{9,10},{10,1... | collective-permute-start | bytes 122888 | tf_op jit(solution)/shard_map/ppermute | solution.py:22
  8.4 2.4 %collective-permute-start = (f32[1,4,2,128]{3,2,1,0:T(2,128)S(1)}, f32[1,4,2,128]{3,2,1,0:T(2,128)S(1)}, u32[]{:S(2)}, u32[]{:S(2)}) collective-permute-start(f32[1,4,2,128]{3,2,1,0:T(2,128)S(1)} %get-tuple-element.559), channel_id=1, source_target_pairs={{0,1},{1,2},{2,3},{3,4},{4,5},{5,6},{6,7},{7,0},{8,9},{9,10},{10,1... | collective-permute-start | bytes 12296 | tf_op jit(solution)/shard_map/ppermute | solution.py:22
  10.8 2.1 %collective-permute-start.1 = (f32[1,4,2,128]{3,2,1,0:T(2,128)S(1)}, f32[1,4,2,128]{3,2,1,0:T(2,128)S(1)}, u32[]{:S(2)}, u32[]{:S(2)}) collective-permute-start(f32[1,4,2,128]{3,2,1,0:T(2,128)S(1)} %get-tuple-element.560), channel_id=1, source_target_pairs={{1,0},{2,1},{3,2},{4,3},{5,4},{6,5},{7,6},{0,7},{9,8},{10,9},{11,1... | collective-permute-start | bytes 12296 | tf_op jit(solution)/shard_map/ppermute | solution.py:25
  16.1 3.8 %collective-permute-start.3 = (f32[1,4,68,2]{3,2,1,0:T(8,128)S(1)}, f32[1,4,68,2]{3,2,1,0:T(8,128)S(1)}, u32[]{:S(2)}, u32[]{:S(2)}) collective-permute-start(f32[1,4,68,2]{3,2,1,0:T(8,128)S(1)} %get-tuple-element.558), channel_id=1, source_target_pairs={{8,0},{16,8},{24,16},{32,24},{40,32},{48,40},{56,48},{64,56},{72,6... | collective-permute-start | bytes 6536 | tf_op jit(solution)/shard_map/ppermute | solution.py:25
  25.7 2.5 %copy.17 = f32[5,8,68,2]{2,1,3,0:T(8,128)} copy(f32[5,8,68,2]{3,2,1,0:T(8,128)} %get-tuple-element.544) | data formatting | bytes 43520 | tf_op jit(solution)/shard_map/slice | solution.py:23
  29.5 3.7 %collective-permute-start.7 = (f32[5,8,68,2]{2,1,3,0:T(8,128)}, f32[5,8,68,2]{2,1,3,0:T(8,128)}, u32[]{:S(2)}, u32[]{:S(2)}) collective-permute-start(f32[5,8,68,2]{2,1,3,0:T(8,128)} %copy.18), channel_id=1, source_target_pairs={{8,0},{16,8},{24,16},{32,24},{40,32},{48,40},{56,48},{64,56},{72,6... | collective-permute-start | bytes 65288 | tf_op jit(solution)/shard_map/ppermute | solution.py:25
  35.5 2.5 %copy.20 = f32[5,8,68,2]{3,2,1,0:T(8,128)} copy(f32[5,8,68,2]{2,1,3,0:T(8,128)} %collective-permute-done.7) | data formatting | bytes 43520 | tf_op jit(solution)/shard_map/ppermute | solution.py:25
  43.8 3.5 %collective-permute-done.9 = f32[80,132]{1,0:T(8,128)S(1)} collective-permute-done((f32[80,132]{1,0:T(8,128)S(1)}, f32[80,132]{1,0:T(8,128)S(1)}, u32[]{:S(2)}, u32[]{:S(2)}) %collective-permute-start.9) | collective-permute-done | bytes 42272 | tf_op jit(solution)/shard_map/ppermute | solution.py:13
  47.4 2.8 %collective-permute-start.10 = (f32[80,132]{1,0:T(8,128)S(1)}, f32[80,132]{1,0:T(8,128)S(1)}, u32[]{:S(2)}, u32[]{:S(2)}) collective-permute-start(f32[80,132]{1,0:T(8,128)S(1)} %collective-permute-done.9), channel_id=1, source_target_pairs={{0,32},{8,40},{16,48},{24,56},{32,0},{40,8},{48,16},{56,24},{64,96... | collective-permute-start | bytes 126728 | tf_op jit(solution)/shard_map/ppermute | solution.py:13
  50.2 3.1 %collective-permute-done.10 = f32[80,132]{1,0:T(8,128)S(1)} collective-permute-done((f32[80,132]{1,0:T(8,128)S(1)}, f32[80,132]{1,0:T(8,128)S(1)}, u32[]{:S(2)}, u32[]{:S(2)}) %collective-permute-start.10) | collective-permute-done | bytes 42272 | tf_op jit(solution)/shard_map/ppermute | solution.py:13
  54.0 2.8 %pad_maximum_fusion.6 = f32[5,8,68,132]{3,2,1,0:T(8,128)S(1)} fusion(f32[5,8,68,2]{3,2,1,0:T(8,128)} %copy.20, f32[5,8,2,128]{3,2,1,0:T(2,128)} %copy-done.6, f32[5,7,64,128]{3,2,1,0:T(8,128)S(1)} %copy-done, f32[5,1,64,128]{3,2,1,0:T(8,128)S(1)} %fusion.117, f32[5,8,2,128]{3,2,1,0:T(2,128)S(1)} %collective-permute-done.4, f32[5,8,68,2]{3,2,1,0:T(8,128)S(1)} %copy.19), kind=kLoop, calls=%fused_computation.290 | loop fusion | flops 1795200 | bytes 2872320 | tf_op jit(solution)/shard_map/concatenate | solution.py:26
  65.3 3.0 %pad_maximum_fusion = f32[5,2,8,66,130]{4,3,2,0,1:T(8,128)} fusion(f32[5,1,8,66,130]{4,3,2,0,1:T(8,128)S(1)} %fusion.99, f32[5,1,8,66,130]{4,3,2,0,1:T(8,128)S(1)} %get-tuple-element.540), kind=kLoop, calls=%fused_computation.272 | loop fusion | flops 686400 | bytes 5491200 | tf_op jit(solution)/shard_map/stack | solution.py:155
  71.4 35.1 %while.28 = (s32[]{:T(128)}, f32[5,8,64,129]{3,2,1,0:T(8,128)}, f32[5,8,65,128]{3,2,1,0:T(8,128)}, f32[64,129]{1,0:T(8,128)S(1)}, f32[5,8,66,130]{3,2,1,0:T(8,12...) while((s32[]{:T(128)}, f32[5,8,64,129]{3,2,1,0:T(8,128)}, ...), condition=%wide.region_1.2_spmd, body=%wide.region_0.1_spmd.sunk | while | flops 6597250 | bytes 30021132 | solution.py:149
  106.6 4.1 %fusion.105 = f32[5,8,64,128]{3,2,1,0:T(8,128)S(1)} fusion(f32[5,1,64,128]{3,2,1,0:T(8,128)S(1)} %fusion.117, f32[5,7,64,128]{3,2,1,0:T(8,128)} %broadcast_multiply_fusion.1, f32[5,8,65,128]{3,2,1,0:T(8,128)} %get-tuple-element.259, f32[5,8,64,129]{3,2,1,0:T(8,128)} %get-tuple-element.258), kind=kLoop, calls=%fused_computation.303 | loop fusion | flops 1638400 | bytes 7864320 | tf_op jit(solution)/shard_map/sub | solution.py:162
  112.0 6.0 %collective-permute-start.12 = (f32[5,8,2,128]{3,2,1,0:T(2,128)S(1)}, f32[5,8,2,128]{3,2,1,0:T(2,128)S(1)}, u32[]{:S(2)}, u32[]{:S(2)}) collective-permute-start(f32[5,8,2,128]{3,2,1,0:T(2,128)S(1)} %get-tuple-element.548), channel_id=1, source_target_pairs={{0,1},{1,2},{2,3},{3,4},{4,5},{5,6},{6,7},{7,0},{8,9},{9,10},{10,1... | collective-permute-start | bytes 122888 | tf_op jit(solution)/shard_map/ppermute | solution.py:22
  119.7 3.8 %collective-permute-done.13 = f32[5,8,2,128]{3,2,1,0:T(2,128)S(1)} collective-permute-done((f32[5,8,2,128]{3,2,1,0:T(2,128)S(1)}, f32[5,8,2,128]{3,2,1,0:T(2,128)S(1)}, u32[]{:S(2)}, u32[]{:S(2)}) %collective-permute-start.13) | collective-permute-done | bytes 40992 | tf_op jit(solution)/shard_map/ppermute | solution.py:25
  127.8 3.9 %collective-permute-start.15 = (f32[5,8,68,2]{2,1,3,0:T(8,128)S(1)}, f32[5,8,68,2]{2,1,3,0:T(8,128)S(1)}, u32[]{:S(2)}, u32[]{:S(2)}) collective-permute-start(f32[5,8,68,2]{2,1,3,0:T(8,128)S(1)} %copy.23), channel_id=1, source_target_pairs={{8,0},{16,8},{24,16},{32,24},{40,32},{48,40},{56,48},{64,56},{72,6... | collective-permute-start | bytes 65288 | tf_op jit(solution)/shard_map/ppermute | solution.py:25
  137.8 4.5 %collective-permute-done.17 = f32[80,132]{1,0:T(8,128)S(1)} collective-permute-done((f32[80,132]{1,0:T(8,128)S(1)}, f32[80,132]{1,0:T(8,128)S(1)}, u32[]{:S(2)}, u32[]{:S(2)}) %collective-permute-start.17) | collective-permute-done | bytes 42272 | tf_op jit(solution)/shard_map/ppermute | solution.py:13
  142.3 2.3 %collective-permute-start.18 = (f32[80,132]{1,0:T(8,128)S(1)}, f32[80,132]{1,0:T(8,128)S(1)}, u32[]{:S(2)}, u32[]{:S(2)}) collective-permute-start(f32[80,132]{1,0:T(8,128)S(1)} %collective-permute-done.17), channel_id=1, source_target_pairs={{0,32},{8,40},{16,48},{24,56},{32,0},{40,8},{48,16},{56,24},{64,96... | collective-permute-start | bytes 126728 | tf_op jit(solution)/shard_map/ppermute | solution.py:13
  144.5 3.7 %collective-permute-done.18 = f32[80,132]{1,0:T(8,128)S(1)} collective-permute-done((f32[80,132]{1,0:T(8,128)S(1)}, f32[80,132]{1,0:T(8,128)S(1)}, u32[]{:S(2)}, u32[]{:S(2)}) %collective-permute-start.18) | collective-permute-done | bytes 42272 | tf_op jit(solution)/shard_map/ppermute | solution.py:13
  149.0 2.8 %pad_maximum_fusion.8 = f32[5,8,68,132]{3,2,1,0:T(8,128)S(1)} fusion(f32[5,8,68,2]{3,2,1,0:T(8,128)} %copy.25, f32[5,8,2,128]{3,2,1,0:T(2,128)S(1)} %collective-permute-done.13, f32[5,7,64,128]{3,2,1,0:T(8,128)S(1)} %get-tuple-element.433, f32[5,1,64,128]{3,2,1,0:T(8,128)S(1)} %get-tuple-element.552, f32[5,8,2,128]{3,2,1,0:T(2,128)S(1)} %collective-permute-done.12, ...), kind=kLoop, calls=%fused_computation.292 | loop fusion | flops 1795200 | bytes 2872320 | tf_op jit(solution)/shard_map/concatenate | solution.py:26
  160.3 3.0 %pad_maximum_fusion.1 = f32[5,2,8,66,130]{4,3,2,0,1:T(8,128)} fusion(f32[5,1,8,66,130]{4,3,2,0,1:T(8,128)S(1)} %fusion.94, f32[5,1,8,66,130]{4,3,2,0,1:T(8,128)S(1)} %get-tuple-element.538), kind=kLoop, calls=%fused_computation.273 | loop fusion | flops 686400 | bytes 5491200 | tf_op jit(solution)/shard_map/stack | solution.py:155
  166.4 35.1 %while.29 = (s32[]{:T(128)}, f32[5,8,64,129]{3,2,1,0:T(8,128)}, f32[5,8,65,128]{3,2,1,0:T(8,128)}, f32[64,129]{1,0:T(8,128)S(1)}, f32[5,8,66,130]{3,2,1,0:T(8,12...) while((s32[]{:T(128)}, f32[5,8,64,129]{3,2,1,0:T(8,128)}, ...), condition=%wide.region_3.4_spmd, body=%wide.region_2.3_spmd.sunk | while | flops 6597250 | bytes 30021132 | solution.py:149
  201.5 4.1 %fusion.103 = f32[5,8,64,128]{3,2,1,0:T(8,128)S(1)} fusion(f32[5,1,64,128]{3,2,1,0:T(8,128)S(1)} %get-tuple-element.552, f32[5,7,64,128]{3,2,1,0:T(8,128)} %get-tuple-element.432, f32[5,8,65,128]{3,2,1,0:T(8,128)} %get-tuple-element.261, f32[5,8,64,129]{3,2,1,0:T(8,128)} %get-tuple-element.260), kind=kLoop, calls=%fused_computation.301 | loop fusion | flops 1638400 | bytes 7864320 | tf_op jit(solution)/shard_map/sub | solution.py:162
  (433 shorter events, 131.1 us)
Async XLA Ops:
  0.6 12.3 %copy-start.8 = (f32[5,64,128]{2,1,0:T(8,128)S(1)}, f32[5,64,128]{2,1,0:T(8,128)}, u32[]{:S(2)}) copy-start(f32[5,64,128]{2,1,0:T(8,128)} %param.11) | copy-start | bytes 491524
  0.6 7.7 %copy-start.10 = (s32[64,128]{1,0:T(8,128)S(1)}, s32[64,128]{1,0:T(8,128)}, u32[]{:S(2)}) copy-start(s32[64,128]{1,0:T(8,128)} %param.15) | copy-start | bytes 98308
  2.7 17.2 %copy-start = (f32[5,7,64,128]{3,2,1,0:T(8,128)S(1)}, f32[5,7,64,128]{3,2,1,0:T(8,128)}, u32[]{:S(2)}) copy-start(f32[5,7,64,128]{3,2,1,0:T(8,128)} %param.12) | copy-start | bytes 3440644
  3.8 20.0 %collective-permute-start.4 = (f32[5,8,2,128]{3,2,1,0:T(2,128)S(1)}, f32[5,8,2,128]{3,2,1,0:T(2,128)S(1)}, u32[]{:S(2)}, u32[]{:S(2)}) collective-permute-start(f32[5,8,2,128]{3,2,1,0:T(2,128)S(1)} %get-tuple-element.553), channel_id=1, source_target_pairs={{0,1},{1,2},{2,3},{3,4},{4,5},{5,6},{6,7},{7,0},{8,9},{9,10},{10,1... | collective-permute-start | bytes 122888 | tf_op jit(solution)/shard_map/ppermute | solution.py:22
  7.1 16.8 %collective-permute-start.5 = (f32[5,8,2,128]{3,2,1,0:T(2,128)S(1)}, f32[5,8,2,128]{3,2,1,0:T(2,128)S(1)}, u32[]{:S(2)}, u32[]{:S(2)}) collective-permute-start(f32[5,8,2,128]{3,2,1,0:T(2,128)S(1)} %get-tuple-element.554), channel_id=1, source_target_pairs={{1,0},{2,1},{3,2},{4,3},{5,4},{6,5},{7,6},{0,7},{9,8},{10,9},{11,1... | collective-permute-start | bytes 122888 | tf_op jit(solution)/shard_map/ppermute | solution.py:25
  8.4 6.1 %collective-permute-start = (f32[1,4,2,128]{3,2,1,0:T(2,128)S(1)}, f32[1,4,2,128]{3,2,1,0:T(2,128)S(1)}, u32[]{:S(2)}, u32[]{:S(2)}) collective-permute-start(f32[1,4,2,128]{3,2,1,0:T(2,128)S(1)} %get-tuple-element.559), channel_id=1, source_target_pairs={{0,1},{1,2},{2,3},{3,4},{4,5},{5,6},{6,7},{7,0},{8,9},{9,10},{10,1... | collective-permute-start | bytes 12296 | tf_op jit(solution)/shard_map/ppermute | solution.py:22
  10.8 5.1 %collective-permute-start.1 = (f32[1,4,2,128]{3,2,1,0:T(2,128)S(1)}, f32[1,4,2,128]{3,2,1,0:T(2,128)S(1)}, u32[]{:S(2)}, u32[]{:S(2)}) collective-permute-start(f32[1,4,2,128]{3,2,1,0:T(2,128)S(1)} %get-tuple-element.560), channel_id=1, source_target_pairs={{1,0},{2,1},{3,2},{4,3},{5,4},{6,5},{7,6},{0,7},{9,8},{10,9},{11,1... | collective-permute-start | bytes 12296 | tf_op jit(solution)/shard_map/ppermute | solution.py:25
  16.0 6.8 %collective-permute-start.2 = (f32[1,4,68,2]{3,2,1,0:T(8,128)S(1)}, f32[1,4,68,2]{3,2,1,0:T(8,128)S(1)}, u32[]{:S(2)}, u32[]{:S(2)}) collective-permute-start(f32[1,4,68,2]{3,2,1,0:T(8,128)S(1)} %get-tuple-element.557), channel_id=1, source_target_pairs={{0,8},{8,16},{16,24},{24,32},{32,40},{40,48},{48,56},{56,64},{64,7... | collective-permute-start | bytes 6536 | tf_op jit(solution)/shard_map/ppermute | solution.py:22
  16.1 6.7 %collective-permute-start.3 = (f32[1,4,68,2]{3,2,1,0:T(8,128)S(1)}, f32[1,4,68,2]{3,2,1,0:T(8,128)S(1)}, u32[]{:S(2)}, u32[]{:S(2)}) collective-permute-start(f32[1,4,68,2]{3,2,1,0:T(8,128)S(1)} %get-tuple-element.558), channel_id=1, source_target_pairs={{8,0},{16,8},{24,16},{32,24},{40,32},{48,40},{56,48},{64,56},{72,6... | collective-permute-start | bytes 6536 | tf_op jit(solution)/shard_map/ppermute | solution.py:25
  23.9 14.0 %copy-start.6 = (f32[5,8,2,128]{3,2,1,0:T(2,128)}, f32[5,8,2,128]{3,2,1,0:T(2,128)S(1)}, u32[]{:S(2)}) copy-start(f32[5,8,2,128]{3,2,1,0:T(2,128)S(1)} %collective-permute-done.5) | copy-start | bytes 122884
  28.2 5.9 %collective-permute-start.6 = (f32[5,8,68,2]{2,1,3,0:T(8,128)}, f32[5,8,68,2]{2,1,3,0:T(8,128)}, u32[]{:S(2)}, u32[]{:S(2)}) collective-permute-start(f32[5,8,68,2]{2,1,3,0:T(8,128)} %copy.17), channel_id=1, source_target_pairs={{0,8},{8,16},{16,24},{24,32},{32,40},{40,48},{48,56},{56,64},{64,7... | collective-permute-start | bytes 65288 | tf_op jit(solution)/shard_map/ppermute | solution.py:22
  29.5 6.0 %collective-permute-start.7 = (f32[5,8,68,2]{2,1,3,0:T(8,128)}, f32[5,8,68,2]{2,1,3,0:T(8,128)}, u32[]{:S(2)}, u32[]{:S(2)}) collective-permute-start(f32[5,8,68,2]{2,1,3,0:T(8,128)} %copy.18), channel_id=1, source_target_pairs={{8,0},{16,8},{24,16},{32,24},{40,32},{48,40},{56,48},{64,56},{72,6... | collective-permute-start | bytes 65288 | tf_op jit(solution)/shard_map/ppermute | solution.py:25
  41.4 1.5 collective-permute-start.8
  42.9 4.5 %collective-permute-start.9 = (f32[80,132]{1,0:T(8,128)S(1)}, f32[80,132]{1,0:T(8,128)S(1)}, u32[]{:S(2)}, u32[]{:S(2)}) collective-permute-start(f32[80,132]{1,0:T(8,128)S(1)} %collective-permute-done.8), channel_id=1, source_target_pairs={{0,16},{8,24},{16,0},{24,8},{32,48},{40,56},{48,32},{56,40},{64,80... | collective-permute-start | bytes 126728 | tf_op jit(solution)/shard_map/ppermute | solution.py:13
  47.4 5.9 %collective-permute-start.10 = (f32[80,132]{1,0:T(8,128)S(1)}, f32[80,132]{1,0:T(8,128)S(1)}, u32[]{:S(2)}, u32[]{:S(2)}) collective-permute-start(f32[80,132]{1,0:T(8,128)S(1)} %collective-permute-done.9), channel_id=1, source_target_pairs={{0,32},{8,40},{16,48},{24,56},{32,0},{40,8},{48,16},{56,24},{64,96... | collective-permute-start | bytes 126728 | tf_op jit(solution)/shard_map/ppermute | solution.py:13
  53.3 5.2 %collective-permute-start.11 = (f32[80,132]{1,0:T(8,128)S(1)}, f32[80,132]{1,0:T(8,128)S(1)}, u32[]{:S(2)}, u32[]{:S(2)}) collective-permute-start(f32[80,132]{1,0:T(8,128)S(1)} %collective-permute-done.10), channel_id=1, source_target_pairs={{0,64},{8,72},{16,80},{24,88},{32,96},{40,104},{48,112},{56,120},{... | collective-permute-start | bytes 126728 | tf_op jit(solution)/shard_map/ppermute | solution.py:13
  112.0 7.7 %collective-permute-start.12 = (f32[5,8,2,128]{3,2,1,0:T(2,128)S(1)}, f32[5,8,2,128]{3,2,1,0:T(2,128)S(1)}, u32[]{:S(2)}, u32[]{:S(2)}) collective-permute-start(f32[5,8,2,128]{3,2,1,0:T(2,128)S(1)} %get-tuple-element.548), channel_id=1, source_target_pairs={{0,1},{1,2},{2,3},{3,4},{4,5},{5,6},{6,7},{7,0},{8,9},{9,10},{10,1... | collective-permute-start | bytes 122888 | tf_op jit(solution)/shard_map/ppermute | solution.py:22
  118.0 5.5 %collective-permute-start.13 = (f32[5,8,2,128]{3,2,1,0:T(2,128)S(1)}, f32[5,8,2,128]{3,2,1,0:T(2,128)S(1)}, u32[]{:S(2)}, u32[]{:S(2)}) collective-permute-start(f32[5,8,2,128]{3,2,1,0:T(2,128)S(1)} %get-tuple-element.549), channel_id=1, source_target_pairs={{1,0},{2,1},{3,2},{4,3},{5,4},{6,5},{7,6},{0,7},{9,8},{10,9},{11,1... | collective-permute-start | bytes 122888 | tf_op jit(solution)/shard_map/ppermute | solution.py:25
  127.2 5.6 %collective-permute-start.14 = (f32[5,8,68,2]{2,1,3,0:T(8,128)S(1)}, f32[5,8,68,2]{2,1,3,0:T(8,128)S(1)}, u32[]{:S(2)}, u32[]{:S(2)}) collective-permute-start(f32[5,8,68,2]{2,1,3,0:T(8,128)S(1)} %copy.22), channel_id=1, source_target_pairs={{0,8},{8,16},{16,24},{24,32},{32,40},{40,48},{48,56},{56,64},{64,7... | collective-permute-start | bytes 65288 | tf_op jit(solution)/shard_map/ppermute | solution.py:22
  127.8 5.6 %collective-permute-start.15 = (f32[5,8,68,2]{2,1,3,0:T(8,128)S(1)}, f32[5,8,68,2]{2,1,3,0:T(8,128)S(1)}, u32[]{:S(2)}, u32[]{:S(2)}) collective-permute-start(f32[5,8,68,2]{2,1,3,0:T(8,128)S(1)} %copy.23), channel_id=1, source_target_pairs={{8,0},{16,8},{24,16},{32,24},{40,32},{48,40},{56,48},{64,56},{72,6... | collective-permute-start | bytes 65288 | tf_op jit(solution)/shard_map/ppermute | solution.py:25
  136.4 1.4 collective-permute-start.16
  137.8 4.5 %collective-permute-start.17 = (f32[80,132]{1,0:T(8,128)S(1)}, f32[80,132]{1,0:T(8,128)S(1)}, u32[]{:S(2)}, u32[]{:S(2)}) collective-permute-start(f32[80,132]{1,0:T(8,128)S(1)} %collective-permute-done.16), channel_id=1, source_target_pairs={{0,16},{8,24},{16,0},{24,8},{32,48},{40,56},{48,32},{56,40},{64,80... | collective-permute-start | bytes 126728 | tf_op jit(solution)/shard_map/ppermute | solution.py:13
  142.3 5.9 %collective-permute-start.18 = (f32[80,132]{1,0:T(8,128)S(1)}, f32[80,132]{1,0:T(8,128)S(1)}, u32[]{:S(2)}, u32[]{:S(2)}) collective-permute-start(f32[80,132]{1,0:T(8,128)S(1)} %collective-permute-done.17), channel_id=1, source_target_pairs={{0,32},{8,40},{16,48},{24,56},{32,0},{40,8},{48,16},{56,24},{64,96... | collective-permute-start | bytes 126728 | tf_op jit(solution)/shard_map/ppermute | solution.py:13
  148.2 5.3 %collective-permute-start.19 = (f32[80,132]{1,0:T(8,128)S(1)}, f32[80,132]{1,0:T(8,128)S(1)}, u32[]{:S(2)}, u32[]{:S(2)}) collective-permute-start(f32[80,132]{1,0:T(8,128)S(1)} %collective-permute-done.18), channel_id=1, source_target_pairs={{0,64},{8,72},{16,80},{24,88},{32,96},{40,104},{48,112},{56,120},{... | collective-permute-start | bytes 126728 | tf_op jit(solution)/shard_map/ppermute | solution.py:13
  (9 other events, 34.8 us)
where the time goes:
time: 209 us; the launch traced here: 208 us
  other arithmetic  95.1 us (46%)
  local copies, waits for them, and re-layouts  46.8 us (22%)
  starting transfers between devices  33.3 us (16%)
  waiting for transfers between devices  29.6 us (14%)
    add x50, other arithmetic, region(): centre_val = values + grad_normal * normal_pos + grad_trans * trans_pos  28.5 us
    dynamic_update_slice x20, other arithmetic, all_fluxes(): return lax.map(per_category, (values, slopes))  18.6 us
    ppermute x8, waiting for transfers between devices, from_partner(): lax.ppermute(shard, axis, [(i, i ^ 1 << apart) for i in range(lax.axis_si...  17.5 us
    ppermute x6, starting transfers between devices, extended_2(): lax.ppermute(lax.slice_in_dim(block, 0, width, axis=dim), axis, backward)  14.8 us
    dynamic_slice x10, local copies, waits for them, and re-layouts, all_fluxes(): return lax.map(per_category, (values, slopes))  13.6 us
    another operation x6, other arithmetic, slope_pair(): return jnp.stack([along_lon, along_lat], axis=1)  12.6 us
    ppermute x6, starting transfers between devices, extended_2(): lax.ppermute(lax.slice_in_dim(block, block.shape[dim] - width, None, axis...  11.9 us
    sub x2, other arithmetic, update(): conserved - (east_flux[..., 1:] - east_flux[..., :-1])  8.22 us
  transfers between devices with their start and end apart: 20, of which 13 were waited for; matrix products, arithmetic and copies ran while one was open for 8% of the time, Pallas kernels for 0%

commit v1 on v0

v1 whole, which is shorter than its diff:
```python
import functools

import jax
import jax.numpy as jnp
from jax import lax
from jax.experimental import pallas as pl
from jax.experimental.pallas import tpu as pltpu
from jax.sharding import PartitionSpec as P

STEPS = 2
NF = 8
FLOOR = 0.1
MESH = pl.DeviceIdType.MESH
BASE = 8
pick = jnp.where


def oriented(get, s, d):
    near = [pick(d, get(n, 1), get(n, -1)) for n in (-1, 0, 1, 2)]
    far = [pick(d, get(n, -1), get(n, 1)) for n in (0, 1)]
    two = [pick(d, get(n, 2), get(n, -2)) for n in (0, 1)]
    h = pick(s, get(0, 0), get(1, 0))
    b = pick(s, get(1, 0), get(0, 0))
    c = pick(s, get(-1, 0), get(2, 0))
    hd = pick(s, near[1], near[2])
    bd = pick(s, near[2], near[1])
    cd = pick(s, near[0], near[3])
    return h, b, c, hd, bd, cd, pick(s, far[0], far[1]), pick(s, two[0], two[1])


def mass_flux(get, geo):
    a, area, x1, x2, off, s, d = geo
    h, b, c, hd, bd, cd, hm, h2 = oriented(get, s, d)
    g = b - c
    w1 = a * (h + g * x1)
    w2 = area * (h + g * x2 + (hd - hm) * off)
    w3 = area * (hd + (bd - cd) * x2 - (h2 - h) * off)
    w2o = w2 * off
    w3o = w3 * off
    flux = w1 - w2 + w3
    ch = w1 - w2 + w3o
    cb = w1 * x1 - w2 * x2
    chd = w3 - w2o
    cbd = w3 * x2
    weights = (pick(s, ch, cb), pick(s, cb, ch), cb, pick(s, chd, cbd), pick(s, cbd, chd), cbd, w2o, w3o)
    return flux, weights


def tracer_flux(get, geo, weights):
    s, d = geo[5], geo[6]
    c0, c1, cb, e0, e1, cbd, chm, ch2 = weights
    total = c0 * get(0, 0) + c1 * get(1, 0) - cb * pick(s, get(-1, 0), get(2, 0))
    total += e0 * pick(d, get(0, 1), get(0, -1)) + e1 * pick(d, get(1, 1), get(1, -1))
    total -= cbd * pick(s, pick(d, get(-1, 1), get(-1, -1)), pick(d, get(2, 1), get(2, -1)))
    total += chm * pick(s, pick(d, get(0, -1), get(0, 1)), pick(d, get(1, -1), get(1, 1)))
    total -= ch2 * pick(s, pick(d, get(0, 2), get(0, -2)), pick(d, get(1, 2), get(1, -2)))
    return total


def edge_geometry(a, low, high, case):
    reach = jnp.abs(a)
    b = pick(case == 2.0, high, low)
    area = pick(case == 0.0, 0.0, 0.5 * a * b)
    return a, area, 0.25 - 0.25 * reach, 0.25 - reach / 6.0, 0.25 - b / 6.0, case


def remember(get):
    seen = {}

    def load(n, t):
        if (n, t) not in seen:
            seen[n, t] = get(n, t)
        return seen[n, t]

    return load


def kernel(nx, ny, ncat, height, breadth,
           mass_hbm, tracer_hbm, u_hbm, v_hbm, ce_hbm, cn_hbm, ice,
           mass_out, tracer_out,
           F, S, X, XM, FN, GF, CI, GE, GN, GS,
           ystage, yrecv, xsend, xrecv, gystage, gyrecv, gxsend, gxrecv,
           in_sem, out_sem, ys_sem, yr_sem, xs_sem, xr_sem, g_sem):
    gx = lax.axis_index("gx")
    gy = lax.axis_index("gy")
    bottom = gy == 0
    top = gy == ny - 1
    inner = gy > 0
    west = {"gx": lax.rem(gx + nx - 1, nx), "gy": gy}
    east = {"gx": lax.rem(gx + 1, nx), "gy": gy}
    south = {"gx": gx, "gy": jnp.maximum(gy - 1, 0)}
    north = {"gx": pick(top, nx - 1 - gx, gx), "gy": pick(top, gy, gy + 1)}
    north_slot = pick(top, 1, 0)
    tiles = height // 8
    rows = height + 2 * BASE
    inside = pl.ds(BASE, height)
    lane = lax.broadcasted_iota(jnp.int32, (8, breadth), 1)

    barrier = pltpu.get_barrier_semaphore()
    for where in (west, east, north):
        pl.semaphore_signal(barrier, inc=1, device_id=where, device_id_type=MESH)

    @pl.when(inner)
    def _():
        pl.semaphore_signal(barrier, inc=1, device_id=south, device_id_type=MESH)

    def load_mass(c):
        return pltpu.make_async_copy(mass_hbm.at[c], F.at[0, c, 0, inside], in_sem.at[0, c])

    def load_tracer(c):
        return pltpu.make_async_copy(tracer_hbm.at[c], F.at[0, c, pl.ds(1, NF - 1), inside], in_sem.at[1, c])

    geo_loads = [
        pltpu.make_async_copy(u_hbm, GF.at[0, inside], in_sem.at[2, 0]),
        pltpu.make_async_copy(v_hbm, GF.at[1, inside], in_sem.at[2, 1]),
        pltpu.make_async_copy(ce_hbm, CI.at[0], in_sem.at[2, 2]),
        pltpu.make_async_copy(cn_hbm, CI.at[1], in_sem.at[2, 3]),
    ]
    for copy in geo_loads:
        copy.start()
    for c in range(ncat):
        load_mass(c).start()
        load_tracer(c).start()

    def remote(src, dst, send, recv, to):
        return pltpu.make_async_remote_copy(src_ref=src, dst_ref=dst, send_sem=send, recv_sem=recv, device_id=to, device_id_type=MESH)

    def y_south(k, c):
        return remote(ystage.at[k, c, 0], yrecv.at[k, c, 1], ys_sem.at[k, c, 0], yr_sem.at[k, c, 1], south)

    def y_north(k, c):
        return remote(ystage.at[k, c, 1], yrecv.at[k, c, north_slot], ys_sem.at[k, c, 1], yr_sem.at[k, c, north_slot], north)

    def y_from(k, c, slot):
        return remote(ystage.at[k, c, slot], yrecv.at[k, c, slot], ys_sem.at[k, c, slot], yr_sem.at[k, c, slot], north)

    def x_west(k, c):
        return remote(xsend.at[k, c], xrecv.at[k, c, 1], xs_sem.at[k, c, 0], xr_sem.at[k, c, 1], west)

    def x_east(k, c):
        return remote(xsend.at[k, c], xrecv.at[k, c, 0], xs_sem.at[k, c, 1], xr_sem.at[k, c, 0], east)

    g_north = remote(gystage, gyrecv, g_sem.at[0], g_sem.at[1], north)
    g_east = remote(gxsend, gxrecv, g_sem.at[2], g_sem.at[3], east)

    def send_y(k, c):
        for f in range(NF):
            ystage[k, c, 0, pl.ds(2 * f, 2)] = F[k, c, f, pl.ds(BASE, 2)]
            ystage[k, c, 1, pl.ds(2 * f, 2)] = F[k, c, f, pl.ds(BASE + height - 2, 2)]

        @pl.when(top)
        def _():
            wide = (2 * NF, breadth)
            back = breadth - 1 - lax.broadcasted_iota(jnp.int32, wide, 1)
            row = lax.broadcasted_iota(jnp.int32, wide, 0)
            edge = jnp.take_along_axis(ystage[k, c, 1], back, axis=1)
            ystage[k, c, 1] = pick(lax.rem(row, 2) == 0, pltpu.roll(edge, 2 * NF - 1, 0), pltpu.roll(edge, 1, 0))

        @pl.when(inner)
        def _():
            y_south(k, c).start()

        y_north(k, c).start()

    def pack(source, target, fields):
        def tile(t, carry):
            packed = pltpu.roll(source(0)[pl.ds(BASE - 2 + 8 * t, 8)], 2, 1)
            for f in range(1, fields):
                moved = pltpu.roll(source(f)[pl.ds(BASE - 2 + 8 * t, 8)], 2 + 4 * f, 1)
                packed = pick(lane >= 4 * f, moved, packed)
            target[pl.ds(pl.multiple_of(8 * t, 8), 8)] = packed
            return carry

        lax.fori_loop(0, tiles + 1, tile, 0)

    def send_x(k, c):
        y_from(k, c, 1).wait_recv()
        for f in range(NF):
            F[k, c, f, pl.ds(BASE + height, 2)] = yrecv[k, c, 1, pl.ds(2 * f, 2)]

        @pl.when(inner)
        def _():
            y_from(k, c, 0).wait_recv()
            for f in range(NF):
                F[k, c, f, pl.ds(BASE - 2, 2)] = yrecv[k, c, 0, pl.ds(2 * f, 2)]

        @pl.when(bottom)
        def _():
            for f in range(NF):
                F[k, c, f, pl.ds(BASE - 2, 2)] = jnp.zeros((2, breadth), jnp.float32)

        pack(lambda f: F.at[k, c, f], xsend.at[k, c], NF)
        x_west(k, c).start()
        x_east(k, c).start()

    for copy in geo_loads:
        copy.wait()
    GF[2, inside] = CI[0].astype(jnp.float32)
    GF[3, inside] = CI[1].astype(jnp.float32)
    for f in range(4):
        gystage[pl.ds(f, 1)] = GF[f, pl.ds(BASE + height - 1, 1)]

    @pl.when(inner)
    def _():
        pl.semaphore_wait(barrier, 4)

    @pl.when(bottom)
    def _():
        pl.semaphore_wait(barrier, 3)

    @pl.when(jnp.logical_not(top))
    def _():
        g_north.start()

    block_rows = height // ice.shape[0]
    block_cols = breadth // ice.shape[1]

    def first(c, carry):
        load_mass(c).wait()
        load_tracer(c).wait()
        for r in range(ice.shape[0]):
            mask = jnp.zeros((block_rows, breadth), jnp.float32)
            wide = lax.broadcasted_iota(jnp.int32, (block_rows, breadth), 1)
            for q in range(ice.shape[1]):
                mask = pick(wide >= q * block_cols, ice[r, q].astype(jnp.float32), mask)
            band = pl.ds(BASE + r * block_rows, block_rows)
            F[0, c, 0, band] = F[0, c, 0, band] * mask
        send_y(0, c)
        return carry

    lax.fori_loop(0, ncat, first, 0)

    @pl.when(inner)
    def _():
        g_north.wait_recv()
        for f in range(4):
            GF[f, pl.ds(BASE - 1, 1)] = gyrecv[pl.ds(f, 1)]

    @pl.when(bottom)
    def _():
        for f in range(4):
            GF[f, pl.ds(BASE - 1, 1)] = jnp.zeros((1, breadth), jnp.float32)

    pack(lambda f: GF.at[f], gxsend, 4)
    g_east.start()

    def second(c, carry):
        send_x(0, c)
        return carry

    lax.fori_loop(0, ncat, second, 0)

    g_east.wait_recv()

    def save(where, at, values):
        for q, value in enumerate(values):
            where[q, at] = value

    def geometry(t, carry):
        here = pl.ds(pl.multiple_of(BASE + 8 * t, 8), 8)
        below = pl.ds(BASE - 1 + 8 * t, 8)
        at = pl.ds(pl.multiple_of(8 * t, 8), 8)
        u, v = GF[0, here], GF[1, here]
        u_below, v_below = GF[0, below], GF[1, below]
        save(GE, at, edge_geometry(0.5 * (u + u_below), jnp.abs(v_below), jnp.abs(v), GF[2, here]))
        mine, lower = gxrecv[pl.ds(2 + 8 * t, 8)], gxrecv[pl.ds(1 + 8 * t, 8)]

        def column(x, f):
            return jnp.broadcast_to(x[:, 4 * f + 1:4 * f + 2], (8, breadth))

        save(GS, at, edge_geometry(0.5 * (column(mine, 0) + column(lower, 0)), jnp.abs(column(lower, 1)), jnp.abs(column(mine, 1)), column(mine, 2)))
        return carry

    lax.fori_loop(0, tiles, geometry, 0)

    def north_geometry(t, carry):
        start = jnp.minimum(8 * t - 1, height - 8)
        here = pl.ds(BASE + start, 8)
        u, v, packed = GF[0, here], GF[1, here], gxrecv[pl.ds(2 + start, 8)]

        def from_west(x, f):
            return pltpu.roll(pick(lane == breadth - 1, pltpu.roll(packed, (breadth - 2 - 4 * f) % breadth, 1), x), 1, 1)

        u_west, v_west = from_west(u, 0), from_west(v, 1)
        save(GN, here, edge_geometry(0.5 * (v + v_west), jnp.abs(u_west), jnp.abs(u), GF[3, here]))
        return carry

    lax.fori_loop(0, tiles + 1, north_geometry, 0)

    def edges(where, at):
        a, area, x1, x2, off, case = (where[q, at] for q in range(6))
        return a, area, x1, x2, off, a > 0.0, case == 2.0

    def advance(k, c):
        def shift(t, carry):
            at = pl.ds(pl.multiple_of(8 * t, 8), 8)
            from_west, from_east, mine = xrecv[k, c, 0, at], xrecv[k, c, 1, at], xsend[k, c, at]
            left = lax.rem(lane, 4) < 2
            halo = pick(left, from_west, from_east)
            strip = pick(left, from_west, mine)
            X[at] = strip
            XM[at] = jnp.take_along_axis(strip, lax.rem(lane, 4), axis=1)
            for f in range(NF):
                value = F[k, c, f, pl.ds(BASE - 2 + 8 * t, 8)]
                side = pltpu.roll(halo, (breadth - 2 - 4 * f) % breadth, 1)
                S[0, f, at] = pltpu.roll(pick(lane >= breadth - 2, side, value), 2, 1)
                S[1, f, at] = pltpu.roll(pick(lane >= breadth - 1, side, value), 1, 1)
                S[2, f, at] = pltpu.roll(pick(lane < 1, side, value), breadth - 1, 1)
                S[3, f, at] = pltpu.roll(pick(lane < 2, side, value), breadth - 2, 1)
            return carry

        lax.fori_loop(0, tiles + 1, shift, 0)

        def reader(f, start):
            def get(row, col):
                if col == 0:
                    return F[k, c, f, pl.ds(BASE + start + row, 8)]
                return S[{-2: 0, -1: 1, 1: 2, 2: 3}[col], f, pl.ds(2 + start + row, 8)]

            return remember(get)

        def turned(get):
            return lambda n, t: get(t, n)

        def north_edges(start):
            at = pl.ds(BASE + start, 8)
            geo = edges(GN, at)
            flux, weights = mass_flux(reader(0, start), geo)
            found = [flux]
            for f in range(1, NF):
                found.append(tracer_flux(reader(f, start), geo, weights))
            for f in range(NF):
                FN[f, at] = found[f]
            return found

        north_edges(-1)

        def tile(t, carry):
            start = pl.multiple_of(8 * t, 8)
            at = pl.ds(start, 8)
            geo = edges(GS, at)

            def strip_reader(where):
                def get(row, col):
                    value = where[pl.ds(2 + start + row, 8)]
                    return value if col == 0 else pltpu.roll(value, (breadth - col) % breadth, 1)

                return remember(get)

            flux, weights = mass_flux(turned(strip_reader(XM)), geo)
            strip = pick(lane < 4, flux, tracer_flux(turned(strip_reader(X)), geo, weights))

            def divergence(f, east_flux):
                edge = pltpu.roll(strip, (breadth - 1 - 4 * f) % breadth, 1)
                return east_flux - pick(lane == 0, edge, pltpu.roll(east_flux, 1, 1))

            norths = north_edges(start)
            geo = edges(GE, at)
            flux, weights = mass_flux(turned(reader(0, start)), geo)
            after = pl.ds(BASE + start, 8)
            before = pl.ds(BASE - 1 + start, 8)
            mass = F[k, c, 0, after]
            new_mass = mass - divergence(0, flux) - (norths[0] - FN[0, before])
            F[k + 1, c, 0, after] = new_mass
            scale = 1.0 / jnp.maximum(new_mass, FLOOR)
            for f in range(1, NF):
                flux = tracer_flux(turned(reader(f, start)), geo, weights)
                amount = mass * F[k, c, f, after] - divergence(f, flux) - (norths[f] - FN[f, before])
                F[k + 1, c, f, after] = amount * scale
            return carry

        lax.fori_loop(0, tiles, tile, 0)

    def x_wait(k, c):
        x_east(k, c).wait_recv()
        x_west(k, c).wait_recv()

    def step_one(c, carry):
        x_wait(0, c)
        advance(0, c)
        send_y(1, c)

        @pl.when(c > 0)
        def _():
            send_x(1, c - 1)

        return carry

    lax.fori_loop(0, ncat, step_one, 0)
    send_x(1, ncat - 1)

    def save_mass(c):
        return pltpu.make_async_copy(F.at[2, c, 0, inside], mass_out.at[c], out_sem.at[0, c])

    def save_tracer(c):
        return pltpu.make_async_copy(F.at[2, c, pl.ds(1, NF - 1), inside], tracer_out.at[c], out_sem.at[1, c])

    def step_two(c, carry):
        x_wait(1, c)
        advance(1, c)
        save_mass(c).start()
        save_tracer(c).start()
        return carry

    lax.fori_loop(0, ncat, step_two, 0)

    @pl.when(jnp.logical_not(top))
    def _():
        g_north.wait_send()

    g_east.wait_send()

    def finish(c, carry):
        for k in range(STEPS):
            @pl.when(inner)
            def _():
                y_south(k, c).wait_send()

            y_north(k, c).wait_send()
            x_west(k, c).wait_send()
            x_east(k, c).wait_send()
        save_mass(c).wait()
        save_tracer(c).wait()
        return carry

    lax.fori_loop(0, ncat, finish, 0)


def solution(mesh):
    nx, ny = mesh.shape["gx"], mesh.shape["gy"]

    def per_device(mass, tracer, uvel, vvel, case_east, case_north, ice):
        ncat, height, breadth = mass.shape
        rows = height + 2 * BASE
        packed = height + 8
        f32 = jnp.float32
        hbm = pl.BlockSpec(memory_space=pl.ANY)
        return pl.pallas_call(
            functools.partial(kernel, nx, ny, ncat, height, breadth),
            out_shape=(jax.ShapeDtypeStruct(mass.shape, f32), jax.ShapeDtypeStruct(tracer.shape, f32)),
            in_specs=[hbm] * 6 + [pl.BlockSpec(memory_space=pltpu.SMEM)],
            out_specs=(hbm, hbm),
            scratch_shapes=[
                pltpu.VMEM((STEPS + 1, ncat, NF, rows, breadth), f32),
                pltpu.VMEM((4, NF, packed, breadth), f32),
                pltpu.VMEM((packed, breadth), f32),
                pltpu.VMEM((packed, breadth), f32),
                pltpu.VMEM((NF, packed, breadth), f32),
                pltpu.VMEM((4, rows, breadth), f32),
                pltpu.VMEM((2, height, breadth), jnp.int32),
                pltpu.VMEM((6, height, breadth), f32),
                pltpu.VMEM((6, packed, breadth), f32),
                pltpu.VMEM((6, height, breadth), f32),
                pltpu.VMEM((STEPS, ncat, 2, 2 * NF, breadth), f32),
                pltpu.VMEM((STEPS, ncat, 2, 2 * NF, breadth), f32),
                pltpu.VMEM((STEPS, ncat, packed, breadth), f32),
                pltpu.VMEM((STEPS, ncat, 2, packed, breadth), f32),
                pltpu.VMEM((8, breadth), f32),
                pltpu.VMEM((8, breadth), f32),
                pltpu.VMEM((packed, breadth), f32),
                pltpu.VMEM((packed, breadth), f32),
                pltpu.SemaphoreType.DMA((3, max(ncat, 4))),
                pltpu.SemaphoreType.DMA((2, ncat)),
                pltpu.SemaphoreType.DMA((STEPS, ncat, 2)),
                pltpu.SemaphoreType.DMA((STEPS, ncat, 2)),
                pltpu.SemaphoreType.DMA((STEPS, ncat, 2)),
                pltpu.SemaphoreType.DMA((STEPS, ncat, 2)),
                pltpu.SemaphoreType.DMA((4,)),
            ],
            compiler_params=pltpu.CompilerParams(collective_id=0, has_side_effects=True),
        )(mass, tracer, uvel, vvel, case_east, case_north, ice)

    placed = (P(None, "gy", "gx"), P(None, None, "gy", "gx")) + (P("gy", "gx"),) * 5
    return jax.shard_map(
        per_device,
        mesh=mesh,
        in_specs=placed,
        out_specs=(P(None, "gy", "gx"), P(None, None, "gy", "gx")),
        check_vma=False,
    )
```

time: 209 us -> 61.4 us (0.29)
  other arithmetic: 95.1 us -> 0 us
  Pallas kernels: 0 us -> 56.6 us
  local copies, waits for them, and re-layouts: 46.8 us -> 3.98 us
  starting transfers between devices: 33.3 us -> 0 us
  waiting for transfers between devices: 29.6 us -> 0 us
    pallas_call x0 -> x1, Pallas kernels: none -> 56.6 us  [per_device(): pl.pallas_call(functools.partial(kernel, nx, ny, ncat, height, breadth),...]
    ppermute x20 -> x0, starting transfers between devices: 33.3 us -> none  [the longest x6 14.8 us: extended_2(): lax.ppermute(lax.slice_in_dim(block, 0, width, axis=dim), axis, backward)]
    ppermute x20 -> x0, waiting for transfers between devices: 29.6 us -> none  [the longest x8 17.5 us: from_partner(): lax.ppermute(shard, axis, [(i, i ^ 1 << apart) for i in range(lax.axis_si...]
    add x52 -> x0, other arithmetic: 28.6 us -> none  [the longest x50 28.5 us: region(): centre_val = values + grad_normal * normal_pos + grad_trans * trans_pos]
    dynamic_update_slice x20 -> x0, other arithmetic: 18.6 us -> none  [all_fluxes(): return lax.map(per_category, (values, slopes))]
    dynamic_slice x10 -> x0, local copies, waits for them, and re-layouts: 13.6 us -> none  [all_fluxes(): return lax.map(per_category, (values, slopes))]
    slice x10 -> x0, local copies, waits for them, and re-layouts: 12.9 us -> none  [the longest x6 7.71 us: extended_2(): lax.slice_in_dim(block, block.shape[dim] - width, None, axis=dim)]
    concatenate x150 -> x0, other arithmetic: 12.6 us -> none  [the longest x5 5.87 us: extended_2(): block = jnp.concatenate([low, block, high], axis=dim)]
  transfers between devices with their start and end apart: 20 -> 0, of which waited for: 13 -> 0; matrix products, arithmetic and copies ran while one was open for 8% -> 0% of each run, Pallas kernels for 0% -> 0%
where the time goes in v1:
time: 61.4 us; the launch traced here: 61.2 us
  Pallas kernels  56.6 us (92%)
  local copies, waits for them, and re-layouts  3.98 us (6%)
  between operations  0.64 us (1%)
    pallas_call x1, Pallas kernels, per_device(): pl.pallas_call(functools.partial(kernel, nx, ny, ncat, height, breadth),...  56.6 us
    unnamed x2, local copies, waits for them, and re-layouts  3.98 us

profile of v1, /device:TPU:6, one launch (start us, length us, event | category | flops | bytes accessed | tf_op | source)
XLA Modules:
  0.0 61.2 jit_solution(18006673842000456965)
XLA Ops:
  0.6 56.6 %shard_map.86 = (f32[5,64,128]{2,1,0:T(8,128)}, f32[5,7,64,128]{3,2,1,0:T(8,128)}) custom-call(f32[5,64,128]{2,1,0:T(8,128)} %mass_hbm.1, f32[5,7,64,128]{3,2,1,0:T(8,128)} %tracer_hbm.1, f32[64,128]{1,0:T(8,128)} %u_hbm.1, f32[64,128]{1,0:T(8,128)} %v_hbm.1, s32[64,128]{1,0:T(8,128)} %ce_hbm.1, s32[64,128]{1,0:T(8,128)} %cn_hbm.1, s32[2,4]{1,0:T(2,128)} %ice.1), custom_call_target="tpu_custom_call" | custom-call | tf_op jit(solution)/shard_map/pallas_call | solution.py:438
  57.2 1.6 %copy.11 = f32[5,64,128]{2,1,0:T(8,128)} copy(f32[5,64,128]{2,1,0:T(8,128)} %get-tuple-element.4) | data formatting | bytes 327680
  58.8 2.4 %copy.12 = f32[5,7,64,128]{3,2,1,0:T(8,128)} copy(f32[5,7,64,128]{3,2,1,0:T(8,128)} %get-tuple-element.5) | data formatting | bytes 2293760

commit v2 on v1

--- a/solution.py
+++ b/solution.py
@@ -10,6 +10,7 @@
 STEPS = 2
 NF = 8
 FLOOR = 0.1
+SHIFTS = (-2, -1, 1, 2)
 MESH = pl.DeviceIdType.MESH
 BASE = 8
 pick = jnp.where
@@ -42,19 +43,24 @@
     cb = w1 * x1 - w2 * x2
     chd = w3 - w2o
     cbd = w3 * x2
-    weights = (pick(s, ch, cb), pick(s, cb, ch), cb, pick(s, chd, cbd), pick(s, cbd, chd), cbd, w2o, w3o)
-    return flux, weights
-
-
-def tracer_flux(get, geo, weights):
-    s, d = geo[5], geo[6]
-    c0, c1, cb, e0, e1, cbd, chm, ch2 = weights
-    total = c0 * get(0, 0) + c1 * get(1, 0) - cb * pick(s, get(-1, 0), get(2, 0))
-    total += e0 * pick(d, get(0, 1), get(0, -1)) + e1 * pick(d, get(1, 1), get(1, -1))
-    total -= cbd * pick(s, pick(d, get(-1, 1), get(-1, -1)), pick(d, get(2, 1), get(2, -1)))
-    total += chm * pick(s, pick(d, get(0, -1), get(0, 1)), pick(d, get(1, -1), get(1, 1)))
-    total -= ch2 * pick(s, pick(d, get(0, 2), get(0, -2)), pick(d, get(1, 2), get(1, -2)))
-    return total
+    zero = jnp.zeros_like(flux)
+    points = {
+        (0, 0): (pick(s, ch, cb), 1),
+        (1, 0): (pick(s, cb, ch), 1),
+        (-1, 0): (pick(s, cb, zero), -1),
+        (2, 0): (pick(s, zero, cb), -1),
+    }
+    e0, e1 = pick(s, chd, cbd), pick(s, cbd, chd)
+    back0, back1 = pick(s, w2o, zero), pick(s, zero, w2o)
+    behind, beyond = pick(s, cbd, zero), pick(s, zero, cbd)
+    far0, far1 = pick(s, w3o, zero), pick(s, zero, w3o)
+    points[0, 1], points[0, -1] = (pick(d, e0, back0), 1), (pick(d, back0, e0), 1)
+    points[1, 1], points[1, -1] = (pick(d, e1, back1), 1), (pick(d, back1, e1), 1)
+    points[-1, 1], points[-1, -1] = (pick(d, behind, zero), -1), (pick(d, zero, behind), -1)
+    points[2, 1], points[2, -1] = (pick(d, beyond, zero), -1), (pick(d, zero, beyond), -1)
+    points[0, 2], points[0, -2] = (pick(d, far0, zero), -1), (pick(d, zero, far0), -1)
+    points[1, 2], points[1, -2] = (pick(d, far1, zero), -1), (pick(d, zero, far1), -1)
+    return flux, points
 
 
 def edge_geometry(a, low, high, case):
@@ -78,9 +84,10 @@
 def kernel(nx, ny, ncat, height, breadth,
            mass_hbm, tracer_hbm, u_hbm, v_hbm, ce_hbm, cn_hbm, ice,
            mass_out, tracer_out,
-           F, S, X, XM, FN, GF, CI, GE, GN, GS,
+           FA, FB, FC, SA, SB, ND, GF, CI, GE, GN, GW,
            ystage, yrecv, xsend, xrecv, gystage, gyrecv, gxsend, gxrecv,
            in_sem, out_sem, ys_sem, yr_sem, xs_sem, xr_sem, g_sem):
+    F = (FA, FB, FC)
     gx = lax.axis_index("gx")
     gy = lax.axis_index("gy")
     bottom = gy == 0
@@ -105,10 +112,10 @@
         pl.semaphore_signal(barrier, inc=1, device_id=south, device_id_type=MESH)
 
     def load_mass(c):
-        return pltpu.make_async_copy(mass_hbm.at[c], F.at[0, c, 0, inside], in_sem.at[0, c])
+        return pltpu.make_async_copy(mass_hbm.at[c], FA.at[c, 0, inside], in_sem.at[0, c])
 
     def load_tracer(c):
-        return pltpu.make_async_copy(tracer_hbm.at[c], F.at[0, c, pl.ds(1, NF - 1), inside], in_sem.at[1, c])
+        return pltpu.make_async_copy(tracer_hbm.at[c], FA.at[c, pl.ds(1, NF - 1), inside], in_sem.at[1, c])
 
     geo_loads = [
         pltpu.make_async_copy(u_hbm, GF.at[0, inside], in_sem.at[2, 0]),
@@ -145,8 +152,8 @@
 
     def send_y(k, c):
         for f in range(NF):
-            ystage[k, c, 0, pl.ds(2 * f, 2)] = F[k, c, f, pl.ds(BASE, 2)]
-            ystage[k, c, 1, pl.ds(2 * f, 2)] = F[k, c, f, pl.ds(BASE + height - 2, 2)]
+            ystage[k, c, 0, pl.ds(2 * f, 2)] = F[k][c, f, pl.ds(BASE, 2)]
+            ystage[k, c, 1, pl.ds(2 * f, 2)] = F[k][c, f, pl.ds(BASE + height - 2, 2)]
 
         @pl.when(top)
         def _():
@@ -176,20 +183,20 @@
     def send_x(k, c):
         y_from(k, c, 1).wait_recv()
         for f in range(NF):
-            F[k, c, f, pl.ds(BASE + height, 2)] = yrecv[k, c, 1, pl.ds(2 * f, 2)]
+            F[k][c, f, pl.ds(BASE + height, 2)] = yrecv[k, c, 1, pl.ds(2 * f, 2)]
 
         @pl.when(inner)
         def _():
             y_from(k, c, 0).wait_recv()
             for f in range(NF):
-                F[k, c, f, pl.ds(BASE - 2, 2)] = yrecv[k, c, 0, pl.ds(2 * f, 2)]
+                F[k][c, f, pl.ds(BASE - 2, 2)] = yrecv[k, c, 0, pl.ds(2 * f, 2)]
 
         @pl.when(bottom)
         def _():
             for f in range(NF):
-                F[k, c, f, pl.ds(BASE - 2, 2)] = jnp.zeros((2, breadth), jnp.float32)
-
-        pack(lambda f: F.at[k, c, f], xsend.at[k, c], NF)
+                F[k][c, f, pl.ds(BASE - 2, 2)] = jnp.zeros((2, breadth), jnp.float32)
+
+        pack(lambda f: F[k].at[c, f], xsend.at[k, c], NF)
         x_west(k, c).start()
         x_east(k, c).start()
 
@@ -224,7 +231,7 @@
             for q in range(ice.shape[1]):
                 mask = pick(wide >= q * block_cols, ice[r, q].astype(jnp.float32), mask)
             band = pl.ds(BASE + r * block_rows, block_rows)
-            F[0, c, 0, band] = F[0, c, 0, band] * mask
+            FA[c, 0, band] = FA[c, 0, band] * mask
         send_y(0, c)
         return carry
 
@@ -255,6 +262,9 @@
     def save(where, at, values):
         for q, value in enumerate(values):
             where[q, at] = value
+
+    def from_west(x, packed, f):
+        return pltpu.roll(pick(lane == breadth - 1, pltpu.roll(packed, (breadth - 2 - 4 * f) % breadth, 1), x), 1, 1)
 
     def geometry(t, carry):
         here = pl.ds(pl.multiple_of(BASE + 8 * t, 8), 8)
@@ -264,11 +274,9 @@
         u_below, v_below = GF[0, below], GF[1, below]
         save(GE, at, edge_geometry(0.5 * (u + u_below), jnp.abs(v_below), jnp.abs(v), GF[2, here]))
         mine, lower = gxrecv[pl.ds(2 + 8 * t, 8)], gxrecv[pl.ds(1 + 8 * t, 8)]
-
-        def column(x, f):
-            return jnp.broadcast_to(x[:, 4 * f + 1:4 * f + 2], (8, breadth))
-
-        save(GS, at, edge_geometry(0.5 * (column(mine, 0) + column(lower, 0)), jnp.abs(column(lower, 1)), jnp.abs(column(mine, 1)), column(mine, 2)))
+        u, u_below = from_west(u, mine, 0), from_west(u_below, lower, 0)
+        v, v_below = from_west(v, mine, 1), from_west(v_below, lower, 1)
+        save(GW, at, edge_geometry(0.5 * (u + u_below), jnp.abs(v_below), jnp.abs(v), from_west(GF[2, here], mine, 2)))
         return carry
 
     lax.fori_loop(0, tiles, geometry, 0)
@@ -278,10 +286,7 @@
         here = pl.ds(BASE + start, 8)
         u, v, packed = GF[0, here], GF[1, here], gxrecv[pl.ds(2 + start, 8)]
 
-        def from_west(x, f):
-            return pltpu.roll(pick(lane == breadth - 1, pltpu.roll(packed, (breadth - 2 - 4 * f) % breadth, 1), x), 1, 1)
-
-        u_west, v_west = from_west(u, 0), from_west(v, 1)
+        u_west, v_west = from_west(u, packed, 0), from_west(v, packed, 1)
         save(GN, here, edge_geometry(0.5 * (v + v_west), jnp.abs(u_west), jnp.abs(u), GF[3, here]))
         return carry
 
@@ -291,82 +296,85 @@
         a, area, x1, x2, off, case = (where[q, at] for q in range(6))
         return a, area, x1, x2, off, a > 0.0, case == 2.0
 
-    def advance(k, c):
-        def shift(t, carry):
-            at = pl.ds(pl.multiple_of(8 * t, 8), 8)
-            from_west, from_east, mine = xrecv[k, c, 0, at], xrecv[k, c, 1, at], xsend[k, c, at]
-            left = lax.rem(lane, 4) < 2
-            halo = pick(left, from_west, from_east)
-            strip = pick(left, from_west, mine)
-            X[at] = strip
-            XM[at] = jnp.take_along_axis(strip, lax.rem(lane, 4), axis=1)
-            for f in range(NF):
-                value = F[k, c, f, pl.ds(BASE - 2 + 8 * t, 8)]
-                side = pltpu.roll(halo, (breadth - 2 - 4 * f) % breadth, 1)
-                S[0, f, at] = pltpu.roll(pick(lane >= breadth - 2, side, value), 2, 1)
-                S[1, f, at] = pltpu.roll(pick(lane >= breadth - 1, side, value), 1, 1)
-                S[2, f, at] = pltpu.roll(pick(lane < 1, side, value), breadth - 1, 1)
-                S[3, f, at] = pltpu.roll(pick(lane < 2, side, value), breadth - 2, 1)
-            return carry
-
-        lax.fori_loop(0, tiles + 1, shift, 0)
-
+    edge_lanes = (lane >= breadth - 2, lane >= breadth - 1, lane < 1, lane < 2)
+    left = lax.rem(lane, 4) < 2
+
+    def shift_tile(k, c, S, t):
+        at = pl.ds(8 * t if isinstance(t, int) else pl.multiple_of(8 * t, 8), 8)
+        halo = pick(left, xrecv[k, c, 0, at], xrecv[k, c, 1, at])
+
+        def piece(f):
+            value = F[k][c, f, pl.ds(BASE - 2 + 8 * t, 8)]
+            side = pltpu.roll(halo, (breadth - 2 - 4 * f) % breadth, 1)
+            for q, shift in enumerate(SHIFTS):
+                S[q, f, at] = pltpu.roll(pick(edge_lanes[q], side, value), -shift % breadth, 1)
+
+        return [functools.partial(piece, f) for f in range(NF)]
+
+    def advance(k, c, S, ahead):
         def reader(f, start):
             def get(row, col):
                 if col == 0:
-                    return F[k, c, f, pl.ds(BASE + start + row, 8)]
-                return S[{-2: 0, -1: 1, 1: 2, 2: 3}[col], f, pl.ds(2 + start + row, 8)]
+                    return F[k][c, f, pl.ds(BASE + start + row, 8)]
+                return S[SHIFTS.index(col), f, pl.ds(2 + start + row, 8)]
 
             return remember(get)
 
-        def turned(get):
-            return lambda n, t: get(t, n)
-
-        def north_edges(start):
+        def north_edges(get, start):
             at = pl.ds(BASE + start, 8)
-            geo = edges(GN, at)
-            flux, weights = mass_flux(reader(0, start), geo)
-            found = [flux]
-            for f in range(1, NF):
-                found.append(tracer_flux(reader(f, start), geo, weights))
-            for f in range(NF):
-                FN[f, at] = found[f]
-            return found
-
-        north_edges(-1)
+            flux, points = mass_flux(get, edges(GN, at))
+            ND[0, at] = flux
+            for q, (value, _) in enumerate(points.values()):
+                ND[1 + q, at] = value
+            return flux, points
+
+        north_edges(reader(0, -1), -1)
+        for work in ahead(tiles):
+            work()
 
         def tile(t, carry):
             start = pl.multiple_of(8 * t, 8)
             at = pl.ds(start, 8)
-            geo = edges(GS, at)
-
-            def strip_reader(where):
-                def get(row, col):
-                    value = where[pl.ds(2 + start + row, 8)]
-                    return value if col == 0 else pltpu.roll(value, (breadth - col) % breadth, 1)
-
-                return remember(get)
-
-            flux, weights = mass_flux(turned(strip_reader(XM)), geo)
-            strip = pick(lane < 4, flux, tracer_flux(turned(strip_reader(X)), geo, weights))
-
-            def divergence(f, east_flux):
-                edge = pltpu.roll(strip, (breadth - 1 - 4 * f) % breadth, 1)
-                return east_flux - pick(lane == 0, edge, pltpu.roll(east_flux, 1, 1))
-
-            norths = north_edges(start)
-            geo = edges(GE, at)
-            flux, weights = mass_flux(turned(reader(0, start)), geo)
             after = pl.ds(BASE + start, 8)
             before = pl.ds(BASE - 1 + start, 8)
-            mass = F[k, c, 0, after]
-            new_mass = mass - divergence(0, flux) - (norths[0] - FN[0, before])
-            F[k + 1, c, 0, after] = new_mass
+            work = ahead(t)
+            get = reader(0, start)
+            mass = get(0, 0)
+            north, north_points = north_edges(get, start)
+            if work:
+                work[0]()
+            east, east_points = mass_flux(lambda n, t: get(t, n), edges(GE, at))
+            west, west_points = mass_flux(lambda n, t: get(t, n - 1), edges(GW, at))
+            total = {(0, 0): mass}
+
+            def add(where, value, sign):
+                if where not in total:
+                    total[where] = value if sign > 0 else -value
+                elif sign > 0:
+                    total[where] = total[where] + value
+                else:
+                    total[where] = total[where] - value
+
+            for (n, q), (value, sign) in west_points.items():
+                add((q, n - 1), value, sign)
+            for i, ((n, q), (_, sign)) in enumerate(north_points.items()):
+                add((n - 1, q), ND[1 + i, before], sign)
+            for (n, q), (value, sign) in east_points.items():
+                add((q, n), value, -sign)
+            for (n, q), (value, sign) in north_points.items():
+                add((n, q), value, -sign)
+            new_mass = mass - (east - west) - (north - ND[0, before])
+            F[k + 1][c, 0, after] = new_mass
             scale = 1.0 / jnp.maximum(new_mass, FLOOR)
             for f in range(1, NF):
-                flux = tracer_flux(turned(reader(f, start)), geo, weights)
-                amount = mass * F[k, c, f, after] - divergence(f, flux) - (norths[f] - FN[f, before])
-                F[k + 1, c, f, after] = amount * scale
+                if work:
+                    work[f]()
+                get = reader(f, start)
+                sums = [None, None]
+                for i, ((row, col), value) in enumerate(total.items()):
+                    term = value * get(row, col)
+                    sums[i % 2] = term if sums[i % 2] is None else sums[i % 2] + term
+                F[k + 1][c, f, after] = (sums[0] + sums[1]) * scale
             return carry
 
         lax.fori_loop(0, tiles, tile, 0)
@@ -375,34 +383,35 @@
         x_east(k, c).wait_recv()
         x_west(k, c).wait_recv()
 
-    def step_one(c, carry):
-        x_wait(0, c)
-        advance(0, c)
-        send_y(1, c)
-
-        @pl.when(c > 0)
-        def _():
-            send_x(1, c - 1)
-
-        return carry
-
-    lax.fori_loop(0, ncat, step_one, 0)
-    send_x(1, ncat - 1)
-
     def save_mass(c):
-        return pltpu.make_async_copy(F.at[2, c, 0, inside], mass_out.at[c], out_sem.at[0, c])
+        return pltpu.make_async_copy(FC.at[c, 0, inside], mass_out.at[c], out_sem.at[0, c])
 
     def save_tracer(c):
-        return pltpu.make_async_copy(F.at[2, c, pl.ds(1, NF - 1), inside], tracer_out.at[c], out_sem.at[1, c])
-
-    def step_two(c, carry):
-        x_wait(1, c)
-        advance(1, c)
-        save_mass(c).start()
-        save_tracer(c).start()
-        return carry
-
-    lax.fori_loop(0, ncat, step_two, 0)
+        return pltpu.make_async_copy(FC.at[c, pl.ds(1, NF - 1), inside], tracer_out.at[c], out_sem.at[1, c])
+
+    order = [(k, c) for k in range(STEPS) for c in range(ncat)]
+    x_wait(0, 0)
+
+    def whole(t, carry):
+        for work in shift_tile(0, 0, SA, t):
+            work()
+        return carry
+
+    lax.fori_loop(0, tiles + 1, whole, 0)
+    for i, (k, c) in enumerate(order):
+        if i + 1 < len(order):
+            x_wait(*order[i + 1])
+            ahead = functools.partial(shift_tile, *order[i + 1], (SA, SB)[(i + 1) % 2])
+        else:
+            ahead = lambda t: []
+        advance(k, c, (SA, SB)[i % 2], ahead)
+        if k == 0:
+            send_y(1, c)
+        else:
+            save_mass(c).start()
+            save_tracer(c).start()
+        if 1 <= i <= ncat:
+            send_x(1, i - 1)
 
     @pl.when(jnp.logical_not(top))
     def _():
@@ -441,11 +450,12 @@
             in_specs=[hbm] * 6 + [pl.BlockSpec(memory_space=pltpu.SMEM)],
             out_specs=(hbm, hbm),
             scratch_shapes=[
-                pltpu.VMEM((STEPS + 1, ncat, NF, rows, breadth), f32),
+                pltpu.VMEM((ncat, NF, rows, breadth), f32),
+                pltpu.VMEM((ncat, NF, rows, breadth), f32),
+                pltpu.VMEM((ncat, NF, rows, breadth), f32),
                 pltpu.VMEM((4, NF, packed, breadth), f32),
-                pltpu.VMEM((packed, breadth), f32),
-                pltpu.VMEM((packed, breadth), f32),
-                pltpu.VMEM((NF, packed, breadth), f32),
+                pltpu.VMEM((4, NF, packed, breadth), f32),
+                pltpu.VMEM((17, packed, breadth), f32),
                 pltpu.VMEM((4, rows, breadth), f32),
                 pltpu.VMEM((2, height, breadth), jnp.int32),
                 pltpu.VMEM((6, height, breadth), f32),

time: 61.4 us -> 48.2 us (0.79)
  Pallas kernels: 56.6 us -> 43 us
    pallas_call x1, Pallas kernels: 56.6 us -> 43 us  [per_device(): pl.pallas_call(functools.partial(kernel, nx, ny, ncat, height, breadth),...]
where the time goes in v2:
time: 48.2 us; the launch traced here: 47.7 us
  Pallas kernels  43 us (89%)
  local copies, waits for them, and re-layouts  3.98 us (8%)
  between operations  0.64 us (1%)
    pallas_call x1, Pallas kernels, per_device(): pl.pallas_call(functools.partial(kernel, nx, ny, ncat, height, breadth),...  43 us
    unnamed x2, local copies, waits for them, and re-layouts  3.98 us

profile of v2, /device:TPU:6, one launch (start us, length us, event | category | flops | bytes accessed | tf_op | source)
XLA Modules:
  0.0 47.7 jit_solution(4299828443780695251)
XLA Ops:
  0.6 43.0 %shard_map.86 = (f32[5,64,128]{2,1,0:T(8,128)}, f32[5,7,64,128]{3,2,1,0:T(8,128)}) custom-call(f32[5,64,128]{2,1,0:T(8,128)} %mass_hbm.1, f32[5,7,64,128]{3,2,1,0:T(8,128)} %tracer_hbm.1, f32[64,128]{1,0:T(8,128)} %u_hbm.1, f32[64,128]{1,0:T(8,128)} %v_hbm.1, s32[64,128]{1,0:T(8,128)} %ce_hbm.1, s32[64,128]{1,0:T(8,128)} %cn_hbm.1, s32[2,4]{1,0:T(2,128)} %ice.1), custom_call_target="tpu_custom_call" | custom-call | tf_op jit(solution)/shard_map/pallas_call | solution.py:447
  43.7 1.6 %copy.11 = f32[5,64,128]{2,1,0:T(8,128)} copy(f32[5,64,128]{2,1,0:T(8,128)} %get-tuple-element.4) | data formatting | bytes 327680
  45.3 2.4 %copy.12 = f32[5,7,64,128]{3,2,1,0:T(8,128)} copy(f32[5,7,64,128]{3,2,1,0:T(8,128)} %get-tuple-element.5) | data formatting | bytes 2293760

commit v3 on v2

--- a/solution.py
+++ b/solution.py
@@ -84,10 +84,10 @@
 def kernel(nx, ny, ncat, height, breadth,
            mass_hbm, tracer_hbm, u_hbm, v_hbm, ce_hbm, cn_hbm, ice,
            mass_out, tracer_out,
-           FA, FB, FC, SA, SB, ND, GF, CI, GE, GN, GW,
+           FA, FB, SA, SB, ND, GF, CI, GE, GN, GW,
            ystage, yrecv, xsend, xrecv, gystage, gyrecv, gxsend, gxrecv,
-           in_sem, out_sem, ys_sem, yr_sem, xs_sem, xr_sem, g_sem):
-    F = (FA, FB, FC)
+           in_sem, ys_sem, yr_sem, xs_sem, xr_sem, g_sem):
+    F = (FA, FB)
     gx = lax.axis_index("gx")
     gy = lax.axis_index("gy")
     bottom = gy == 0
@@ -169,16 +169,23 @@
 
         y_north(k, c).start()
 
-    def pack(source, target, fields):
+    def packed(values):
+        found = pltpu.roll(values[0], 2, 1)
+        for f in range(1, len(values)):
+            found = pick(lane >= 4 * f, pltpu.roll(values[f], 2 + 4 * f, 1), found)
+        return found
+
+    def pack(source, target, fields, first, count):
         def tile(t, carry):
-            packed = pltpu.roll(source(0)[pl.ds(BASE - 2 + 8 * t, 8)], 2, 1)
-            for f in range(1, fields):
-                moved = pltpu.roll(source(f)[pl.ds(BASE - 2 + 8 * t, 8)], 2 + 4 * f, 1)
-                packed = pick(lane >= 4 * f, moved, packed)
-            target[pl.ds(pl.multiple_of(8 * t, 8), 8)] = packed
+            at = first + 8 * t
+            target[pl.ds(2 + at, 8)] = packed([source(f)[pl.ds(BASE + at, 8)] for f in range(fields)])
             return carry
 
-        lax.fori_loop(0, tiles + 1, tile, 0)
+        lax.fori_loop(0, count, tile, 0, unroll=4 if count % 4 == 0 else 3)
+
+    def pack_rim(k, c):
+        for at in (-2, height - 6):
+            xsend[k, c, pl.ds(2 + at, 8)] = packed([F[k][c, f, pl.ds(BASE + at, 8)] for f in range(NF)])
 
     def send_x(k, c):
         y_from(k, c, 1).wait_recv()
@@ -196,7 +203,7 @@
             for f in range(NF):
                 F[k][c, f, pl.ds(BASE - 2, 2)] = jnp.zeros((2, breadth), jnp.float32)
 
-        pack(lambda f: F[k].at[c, f], xsend.at[k, c], NF)
+        pack_rim(k, c)
         x_west(k, c).start()
         x_east(k, c).start()
 
@@ -237,6 +244,12 @@
 
     lax.fori_loop(0, ncat, first, 0)
 
+    def columns(c, carry):
+        pack(lambda f: FA.at[c, f], xsend.at[0, c], NF, 0, tiles)
+        return carry
+
+    lax.fori_loop(0, ncat, columns, 0)
+
     @pl.when(inner)
     def _():
         g_north.wait_recv()
@@ -248,7 +261,7 @@
         for f in range(4):
             GF[f, pl.ds(BASE - 1, 1)] = jnp.zeros((1, breadth), jnp.float32)
 
-    pack(lambda f: GF.at[f], gxsend, 4)
+    pack(lambda f: GF.at[f], gxsend, 4, -2, tiles + 1)
     g_east.start()
 
     def second(c, carry):
@@ -257,7 +270,6 @@
 
     lax.fori_loop(0, ncat, second, 0)
 
-    g_east.wait_recv()
 
     def save(where, at, values):
         for q, value in enumerate(values):
@@ -273,13 +285,24 @@
         u, v = GF[0, here], GF[1, here]
         u_below, v_below = GF[0, below], GF[1, below]
         save(GE, at, edge_geometry(0.5 * (u + u_below), jnp.abs(v_below), jnp.abs(v), GF[2, here]))
+        return carry
+
+    lax.fori_loop(0, tiles, geometry, 0, unroll=2)
+    g_east.wait_recv()
+
+    def west_geometry(t, carry):
+        here = pl.ds(pl.multiple_of(BASE + 8 * t, 8), 8)
+        below = pl.ds(BASE - 1 + 8 * t, 8)
+        at = pl.ds(pl.multiple_of(8 * t, 8), 8)
+        u, v = GF[0, here], GF[1, here]
+        u_below, v_below = GF[0, below], GF[1, below]
         mine, lower = gxrecv[pl.ds(2 + 8 * t, 8)], gxrecv[pl.ds(1 + 8 * t, 8)]
         u, u_below = from_west(u, mine, 0), from_west(u_below, lower, 0)
         v, v_below = from_west(v, mine, 1), from_west(v_below, lower, 1)
         save(GW, at, edge_geometry(0.5 * (u + u_below), jnp.abs(v_below), jnp.abs(v), from_west(GF[2, here], mine, 2)))
         return carry
 
-    lax.fori_loop(0, tiles, geometry, 0)
+    lax.fori_loop(0, tiles, west_geometry, 0, unroll=2)
 
     def north_geometry(t, carry):
         start = jnp.minimum(8 * t - 1, height - 8)
@@ -290,7 +313,7 @@
         save(GN, here, edge_geometry(0.5 * (v + v_west), jnp.abs(u_west), jnp.abs(u), GF[3, here]))
         return carry
 
-    lax.fori_loop(0, tiles + 1, north_geometry, 0)
+    lax.fori_loop(0, tiles + 1, north_geometry, 0, unroll=3)
 
     def edges(where, at):
         a, area, x1, x2, off, case = (where[q, at] for q in range(6))
@@ -347,6 +370,15 @@
             west, west_points = mass_flux(lambda n, t: get(t, n - 1), edges(GW, at))
             total = {(0, 0): mass}
 
+            def emit(f, value):
+                if k + 1 < STEPS:
+                    F[k + 1][c, f, after] = value
+                elif f:
+                    tracer_out[c, f - 1, at] = value
+                else:
+                    mass_out[c, at] = value
+
+
             def add(where, value, sign):
                 if where not in total:
                     total[where] = value if sign > 0 else -value
@@ -364,7 +396,7 @@
             for (n, q), (value, sign) in north_points.items():
                 add((n, q), value, -sign)
             new_mass = mass - (east - west) - (north - ND[0, before])
-            F[k + 1][c, 0, after] = new_mass
+            emit(0, new_mass)
             scale = 1.0 / jnp.maximum(new_mass, FLOOR)
             for f in range(1, NF):
                 if work:
@@ -374,21 +406,17 @@
                 for i, ((row, col), value) in enumerate(total.items()):
                     term = value * get(row, col)
                     sums[i % 2] = term if sums[i % 2] is None else sums[i % 2] + term
-                F[k + 1][c, f, after] = (sums[0] + sums[1]) * scale
+                emit(f, (sums[0] + sums[1]) * scale)
             return carry
 
         lax.fori_loop(0, tiles, tile, 0)
+        if k + 1 < STEPS:
+            pack(lambda f: F[k + 1].at[c, f], xsend.at[k + 1, c], NF, 0, tiles)
 
     def x_wait(k, c):
         x_east(k, c).wait_recv()
         x_west(k, c).wait_recv()
 
-    def save_mass(c):
-        return pltpu.make_async_copy(FC.at[c, 0, inside], mass_out.at[c], out_sem.at[0, c])
-
-    def save_tracer(c):
-        return pltpu.make_async_copy(FC.at[c, pl.ds(1, NF - 1), inside], tracer_out.at[c], out_sem.at[1, c])
-
     order = [(k, c) for k in range(STEPS) for c in range(ncat)]
     x_wait(0, 0)
 
@@ -397,7 +425,7 @@
             work()
         return carry
 
-    lax.fori_loop(0, tiles + 1, whole, 0)
+    lax.fori_loop(0, tiles + 1, whole, 0, unroll=3)
     for i, (k, c) in enumerate(order):
         if i + 1 < len(order):
             x_wait(*order[i + 1])
@@ -407,9 +435,6 @@
         advance(k, c, (SA, SB)[i % 2], ahead)
         if k == 0:
             send_y(1, c)
-        else:
-            save_mass(c).start()
-            save_tracer(c).start()
         if 1 <= i <= ncat:
             send_x(1, i - 1)
 
@@ -428,8 +453,6 @@
             y_north(k, c).wait_send()
             x_west(k, c).wait_send()
             x_east(k, c).wait_send()
-        save_mass(c).wait()
-        save_tracer(c).wait()
         return carry
 
     lax.fori_loop(0, ncat, finish, 0)
@@ -446,11 +469,10 @@
         hbm = pl.BlockSpec(memory_space=pl.ANY)
         return pl.pallas_call(
             functools.partial(kernel, nx, ny, ncat, height, breadth),
-            out_shape=(jax.ShapeDtypeStruct(mass.shape, f32), jax.ShapeDtypeStruct(tracer.shape, f32)),
+            out_shape=(pltpu.VMEM(mass.shape, f32), pltpu.VMEM(tracer.shape, f32)),
             in_specs=[hbm] * 6 + [pl.BlockSpec(memory_space=pltpu.SMEM)],
-            out_specs=(hbm, hbm),
+            out_specs=(pl.BlockSpec(memory_space=pltpu.VMEM),) * 2,
             scratch_shapes=[
-                pltpu.VMEM((ncat, NF, rows, breadth), f32),
                 pltpu.VMEM((ncat, NF, rows, breadth), f32),
                 pltpu.VMEM((ncat, NF, rows, breadth), f32),
                 pltpu.VMEM((4, NF, packed, breadth), f32),
@@ -470,7 +492,6 @@
                 pltpu.VMEM((packed, breadth), f32),
                 pltpu.VMEM((packed, breadth), f32),
                 pltpu.SemaphoreType.DMA((3, max(ncat, 4))),
-                pltpu.SemaphoreType.DMA((2, ncat)),
                 pltpu.SemaphoreType.DMA((STEPS, ncat, 2)),
                 pltpu.SemaphoreType.DMA((STEPS, ncat, 2)),
                 pltpu.SemaphoreType.DMA((STEPS, ncat, 2)),

time: 48.2 us -> 41.4 us (0.86)
  Pallas kernels: 43 us -> 39 us
  local copies, waits for them, and re-layouts: 3.98 us -> 1.67 us
    pallas_call x1, Pallas kernels: 43 us -> 39 us  [per_device(): pl.pallas_call(functools.partial(kernel, nx, ny, ncat, height, breadth),...]
    unnamed x2, local copies, waits for them, and re-layouts: 3.98 us -> 1.67 us
where the time goes in v3:
time: 41.4 us; the launch traced here: 41.3 us
  Pallas kernels  39 us (94%)
  local copies, waits for them, and re-layouts  1.67 us (4%)
  between operations  0.64 us (2%)
    pallas_call x1, Pallas kernels, per_device(): pl.pallas_call(functools.partial(kernel, nx, ny, ncat, height, breadth),...  39 us
    unnamed x2, local copies, waits for them, and re-layouts  1.67 us

profile of v3, /device:TPU:6, one launch (start us, length us, event | category | flops | bytes accessed | tf_op | source)
XLA Modules:
  0.0 41.3 jit_solution(10756626240767802346)
XLA Ops:
  0.6 39.0 %shard_map.86 = (f32[5,64,128]{2,1,0:T(8,128)S(1)}, f32[5,7,64,128]{3,2,1,0:T(8,128)S(1)}) custom-call(f32[5,64,128]{2,1,0:T(8,128)} %mass_hbm.1, f32[5,7,64,128]{3,2,1,0:T(8,128)} %tracer_hbm.1, f32[64,128]{1,0:T(8,128)} %u_hbm.1, f32[64,128]{1,0:T(8,128)} %v_hbm.1, s32[64,128]{1,0:T(8,128)} %ce_hbm.1, s32[64,128]{1,0:T(8,128)} %cn_hbm.1, s32[2,4]{1,0:T(2,128)} %ice.1), custom_call_target="tpu_custom_call" | custom-call | tf_op jit(solution)/shard_map/pallas_call | solution.py:470
  39.6 0.7 %copy.11 = f32[5,64,128]{2,1,0:T(8,128)} copy(f32[5,64,128]{2,1,0:T(8,128)S(1)} %get-tuple-element.2) | data formatting | bytes 327680
  40.3 1.0 %copy.12 = f32[5,7,64,128]{3,2,1,0:T(8,128)} copy(f32[5,7,64,128]{3,2,1,0:T(8,128)S(1)} %get-tuple-element.3) | data formatting | bytes 2293760

commit v4 on v3

--- a/solution.py
+++ b/solution.py
@@ -334,7 +334,7 @@
 
         return [functools.partial(piece, f) for f in range(NF)]
 
-    def advance(k, c, S, ahead):
+    def advance(k, c, S, ahead, between):
         def reader(f, start):
             def get(row, col):
                 if col == 0:
@@ -409,7 +409,12 @@
                 emit(f, (sums[0] + sums[1]) * scale)
             return carry
 
-        lax.fori_loop(0, tiles, tile, 0)
+        if between is None:
+            lax.fori_loop(0, tiles, tile, 0)
+        else:
+            lax.fori_loop(0, tiles // 2, tile, 0)
+            send_x(1, between)
+            lax.fori_loop(tiles // 2, tiles, tile, 0)
         if k + 1 < STEPS:
             pack(lambda f: F[k + 1].at[c, f], xsend.at[k + 1, c], NF, 0, tiles)
 
@@ -427,16 +432,26 @@
 
     lax.fori_loop(0, tiles + 1, whole, 0, unroll=3)
     for i, (k, c) in enumerate(order):
-        if i + 1 < len(order):
+        if i + 1 < ncat:
             x_wait(*order[i + 1])
             ahead = functools.partial(shift_tile, *order[i + 1], (SA, SB)[(i + 1) % 2])
         else:
             ahead = lambda t: []
-        advance(k, c, (SA, SB)[i % 2], ahead)
+        advance(k, c, (SA, SB)[i % 2], ahead, None)
+        if 2 <= i < ncat + 2:
+            send_x(1, i - 2)
+        if ncat <= i + 1 < len(order):
+            x_wait(*order[i + 1])
+            nxt = order[i + 1]
+
+            def whole(t, carry, nxt=nxt, S=(SA, SB)[(i + 1) % 2]):
+                for work in shift_tile(*nxt, S, t):
+                    work()
+                return carry
+
+            lax.fori_loop(0, tiles + 1, whole, 0, unroll=3)
         if k == 0:
             send_y(1, c)
-        if 1 <= i <= ncat:
-            send_x(1, i - 1)
 
     @pl.when(jnp.logical_not(top))
     def _():

time: 41.4 us -> 37 us (0.89)
  Pallas kernels: 39 us -> 34.6 us
    pallas_call x1, Pallas kernels: 39 us -> 34.6 us  [per_device(): pl.pallas_call(functools.partial(kernel, nx, ny, ncat, height, breadth),...]
where the time goes in v4:
time: 37 us; the launch traced here: 36.9 us
  Pallas kernels  34.6 us (94%)
  local copies, waits for them, and re-layouts  1.67 us (5%)
  between operations  0.64 us (2%)
    pallas_call x1, Pallas kernels, per_device(): pl.pallas_call(functools.partial(kernel, nx, ny, ncat, height, breadth),...  34.6 us
    unnamed x2, local copies, waits for them, and re-layouts  1.67 us

profile of v4, /device:TPU:6, one launch (start us, length us, event | category | flops | bytes accessed | tf_op | source)
XLA Modules:
  0.0 36.9 jit_solution(13309393323400464016)
XLA Ops:
  0.6 34.6 %shard_map.86 = (f32[5,64,128]{2,1,0:T(8,128)S(1)}, f32[5,7,64,128]{3,2,1,0:T(8,128)S(1)}) custom-call(f32[5,64,128]{2,1,0:T(8,128)} %mass_hbm.1, f32[5,7,64,128]{3,2,1,0:T(8,128)} %tracer_hbm.1, f32[64,128]{1,0:T(8,128)} %u_hbm.1, f32[64,128]{1,0:T(8,128)} %v_hbm.1, s32[64,128]{1,0:T(8,128)} %ce_hbm.1, s32[64,128]{1,0:T(8,128)} %cn_hbm.1, s32[2,4]{1,0:T(2,128)} %ice.1), custom_call_target="tpu_custom_call" | custom-call | tf_op jit(solution)/shard_map/pallas_call | solution.py:485
  35.2 0.7 %copy.11 = f32[5,64,128]{2,1,0:T(8,128)} copy(f32[5,64,128]{2,1,0:T(8,128)S(1)} %get-tuple-element.2) | data formatting | bytes 327680
  35.9 1.0 %copy.12 = f32[5,7,64,128]{3,2,1,0:T(8,128)} copy(f32[5,7,64,128]{3,2,1,0:T(8,128)S(1)} %get-tuple-element.3) | data formatting | bytes 2293760

commit v5 on v4

--- a/solution.py
+++ b/solution.py
@@ -334,7 +334,7 @@
 
         return [functools.partial(piece, f) for f in range(NF)]
 
-    def advance(k, c, S, ahead, between):
+    def advance(k, c, S, ahead):
         def reader(f, start):
             def get(row, col):
                 if col == 0:
@@ -409,14 +409,13 @@
                 emit(f, (sums[0] + sums[1]) * scale)
             return carry
 
-        if between is None:
-            lax.fori_loop(0, tiles, tile, 0)
+        if k + 1 < STEPS:
+            north_edges(reader(0, height - 9), height - 9)
+            lax.fori_loop(0, 2, lambda i, carry: tile((tiles - 1) * i, carry), 0)
+            send_y(k + 1, c)
+            lax.fori_loop(1, tiles - 1, tile, 0)
         else:
-            lax.fori_loop(0, tiles // 2, tile, 0)
-            send_x(1, between)
-            lax.fori_loop(tiles // 2, tiles, tile, 0)
-        if k + 1 < STEPS:
-            pack(lambda f: F[k + 1].at[c, f], xsend.at[k + 1, c], NF, 0, tiles)
+            lax.fori_loop(0, tiles, tile, 0, unroll=1 if ahead(0) else 4)
 
     def x_wait(k, c):
         x_east(k, c).wait_recv()
@@ -437,7 +436,7 @@
             ahead = functools.partial(shift_tile, *order[i + 1], (SA, SB)[(i + 1) % 2])
         else:
             ahead = lambda t: []
-        advance(k, c, (SA, SB)[i % 2], ahead, None)
+        advance(k, c, (SA, SB)[i % 2], ahead)
         if 2 <= i < ncat + 2:
             send_x(1, i - 2)
         if ncat <= i + 1 < len(order):
@@ -451,7 +450,7 @@
 
             lax.fori_loop(0, tiles + 1, whole, 0, unroll=3)
         if k == 0:
-            send_y(1, c)
+            pack(lambda f: FB.at[c, f], xsend.at[1, c], NF, 0, tiles)
 
     @pl.when(jnp.logical_not(top))
     def _():

time: 37 us -> 35 us (0.946)
  Pallas kernels: 34.6 us -> 32.5 us
    pallas_call x1, Pallas kernels: 34.6 us -> 32.5 us  [per_device(): pl.pallas_call(functools.partial(kernel, nx, ny, ncat, height, breadth),...]
where the time goes in v5:
time: 35 us; the launch traced here: 34.9 us
  Pallas kernels  32.5 us (93%)
  local copies, waits for them, and re-layouts  1.67 us (5%)
  between operations  0.64 us (2%)
    pallas_call x1, Pallas kernels, per_device(): pl.pallas_call(functools.partial(kernel, nx, ny, ncat, height, breadth),...  32.5 us
    unnamed x2, local copies, waits for them, and re-layouts  1.67 us

profile of v5, /device:TPU:6, one launch (start us, length us, event | category | flops | bytes accessed | tf_op | source)
XLA Modules:
  0.0 34.9 jit_solution(16290875088248619277)
XLA Ops:
  0.6 32.5 %shard_map.86 = (f32[5,64,128]{2,1,0:T(8,128)S(1)}, f32[5,7,64,128]{3,2,1,0:T(8,128)S(1)}) custom-call(f32[5,64,128]{2,1,0:T(8,128)} %mass_hbm.1, f32[5,7,64,128]{3,2,1,0:T(8,128)} %tracer_hbm.1, f32[64,128]{1,0:T(8,128)} %u_hbm.1, f32[64,128]{1,0:T(8,128)} %v_hbm.1, s32[64,128]{1,0:T(8,128)} %ce_hbm.1, s32[64,128]{1,0:T(8,128)} %cn_hbm.1, s32[2,4]{1,0:T(2,128)} %ice.1), custom_call_target="tpu_custom_call" | custom-call | tf_op jit(solution)/shard_map/pallas_call | solution.py:484
  33.2 0.7 %copy.11 = f32[5,64,128]{2,1,0:T(8,128)} copy(f32[5,64,128]{2,1,0:T(8,128)S(1)} %get-tuple-element.2) | data formatting | bytes 327680
  33.9 1.0 %copy.12 = f32[5,7,64,128]{3,2,1,0:T(8,128)} copy(f32[5,7,64,128]{3,2,1,0:T(8,128)S(1)} %get-tuple-element.3) | data formatting | bytes 2293760

commit v6 on v5

--- a/solution.py
+++ b/solution.py
@@ -411,9 +411,9 @@
 
         if k + 1 < STEPS:
             north_edges(reader(0, height - 9), height - 9)
-            lax.fori_loop(0, 2, lambda i, carry: tile((tiles - 1) * i, carry), 0)
+            lax.fori_loop(0, 2, lambda i, carry: tile((tiles - 1) * i, carry), 0, unroll=2)
             send_y(k + 1, c)
-            lax.fori_loop(1, tiles - 1, tile, 0)
+            lax.fori_loop(1, tiles - 1, tile, 0, unroll=3)
         else:
             lax.fori_loop(0, tiles, tile, 0, unroll=1 if ahead(0) else 4)
 
@@ -431,7 +431,7 @@
 
     lax.fori_loop(0, tiles + 1, whole, 0, unroll=3)
     for i, (k, c) in enumerate(order):
-        if i + 1 < ncat:
+        if False:
             x_wait(*order[i + 1])
             ahead = functools.partial(shift_tile, *order[i + 1], (SA, SB)[(i + 1) % 2])
         else:
@@ -439,7 +439,7 @@
         advance(k, c, (SA, SB)[i % 2], ahead)
         if 2 <= i < ncat + 2:
             send_x(1, i - 2)
-        if ncat <= i + 1 < len(order):
+        if i + 1 < len(order):
             x_wait(*order[i + 1])
             nxt = order[i + 1]
 

time: 35 us -> 34 us (0.971)
  Pallas kernels: 32.5 us -> 31.6 us
    pallas_call x1, Pallas kernels: 32.5 us -> 31.6 us  [per_device(): pl.pallas_call(functools.partial(kernel, nx, ny, ncat, height, breadth),...]
where the time goes in v6:
time: 34 us; the launch traced here: 33.9 us
  Pallas kernels  31.6 us (93%)
  local copies, waits for them, and re-layouts  1.67 us (5%)
  between operations  0.64 us (2%)
    pallas_call x1, Pallas kernels, per_device(): pl.pallas_call(functools.partial(kernel, nx, ny, ncat, height, breadth),...  31.6 us
    unnamed x2, local copies, waits for them, and re-layouts  1.67 us

profile of v6, /device:TPU:6, one launch (start us, length us, event | category | flops | bytes accessed | tf_op | source)
XLA Modules:
  0.0 33.9 jit_solution(14154756250385047993)
XLA Ops:
  0.6 31.6 %shard_map.86 = (f32[5,64,128]{2,1,0:T(8,128)S(1)}, f32[5,7,64,128]{3,2,1,0:T(8,128)S(1)}) custom-call(f32[5,64,128]{2,1,0:T(8,128)} %mass_hbm.1, f32[5,7,64,128]{3,2,1,0:T(8,128)} %tracer_hbm.1, f32[64,128]{1,0:T(8,128)} %u_hbm.1, f32[64,128]{1,0:T(8,128)} %v_hbm.1, s32[64,128]{1,0:T(8,128)} %ce_hbm.1, s32[64,128]{1,0:T(8,128)} %cn_hbm.1, s32[2,4]{1,0:T(2,128)} %ice.1), custom_call_target="tpu_custom_call" | custom-call | tf_op jit(solution)/shard_map/pallas_call | solution.py:484
  32.2 0.7 %copy.11 = f32[5,64,128]{2,1,0:T(8,128)} copy(f32[5,64,128]{2,1,0:T(8,128)S(1)} %get-tuple-element.2) | data formatting | bytes 327680
  32.9 1.0 %copy.12 = f32[5,7,64,128]{3,2,1,0:T(8,128)} copy(f32[5,7,64,128]{3,2,1,0:T(8,128)S(1)} %get-tuple-element.3) | data formatting | bytes 2293760
